TPU v7x, 32 devices: a whole 2x2x4 slice. The times are simulated.
32 devices in a mesh: tilt: 4 (over z), tile: 8 (over y, x, core).
Axes of the slice: x: 2, y: 2, z: 4, core: 2. Of those that a mesh axis runs over, the one named last changes fastest.
Arguments:
- volumes: bfloat16 [48, 128, 64, 128], P('tile', 'tilt'), may hold values from -0.75 to 0.75
- angles: float32 [8], replicated, may hold values from -1.05 to 1.05
- defocus: float32 [8], P('tilt'), may hold values from 0.01 to 0.1
- row_offsets: int32 [48, 8], P('tile', 'tilt'), may hold values from 0 to 1023, as said below
- col_offsets: int32 [48, 8], P('tile', 'tilt'), may hold values from 0 to 128
- measured: float32 [8, 1024, 256], P('tilt', 'tile'), may hold values from -6 to 6
Outputs:
- residual: float32 [8, 1024, 256], P('tilt', 'tile')
- volume_step: float32 [48, 128, 64, 128], P('tile', 'tilt')
Inputs may be any that keep to these rules, and one draw needn't show every extreme that they name: row_offsets[b, t] // 128 is the strip that holds the window's top row. Among the 6 boxes of one index of tile and the 2 tilts of one index of tilt, at most 2 windows have their top row in the same strip; in every draw, for every index of tilt, one strip receives exactly 2 such windows from every index of tile.
All inputs are finite; a program needn't handle non-finite values.
Results may differ from a plain program's by a relative error of at most 0.0047.
Values may be sent and summed in bfloat16 or wider, within the bound.
No kernel may reach another device: no remote copies, remote signals or barrier semaphores. Data moves between devices by JAX's collectives and lax.ppermute only.
A program may use at most 64 MiB of HBM per device.

v0:
```python
import functools

import jax
import jax.numpy as jnp
from jax import lax
from jax.experimental import pallas as pl
from jax.experimental.pallas import tpu as pltpu
from jax.sharding import PartitionSpec as P

HR = 8
REACH = 2 * HR
BF = jnp.bfloat16
F32 = jnp.float32
ABSENT = -1024
GRANT = pltpu.CompilerParams(vmem_limit_bytes=32 * 1024 * 1024)


def ring(block, axis, distance):
    count = lax.axis_size(axis)
    return lax.ppermute(block, axis, [(i, (i + distance) % count) for i in range(count)])


def near(block):
    return pltpu.with_memory_space_constraint(block, pltpu.VMEM)


def quotient(value, size):
    if size & (size - 1) == 0:
        return lax.shift_right_logical(value, size.bit_length() - 1)
    return lax.div(value, size)


def ones_where(mask):
    return jnp.where(mask, jnp.ones(mask.shape, BF), jnp.zeros(mask.shape, BF))


def iota_apart(shape, plus, minus):
    ahead = lax.broadcasted_iota(jnp.int32, shape, plus)
    behind = lax.broadcasted_iota(jnp.int32, shape, minus)
    return (ahead - behind).astype(F32).astype(BF)


def note_sines(angle_ref, sine_ref):
    for t in range(sine_ref.shape[0]):
        sine_ref[t] = jnp.sin(jnp.full(sine_ref.shape[1:], angle_ref[t], F32))


def tap_block(apart, sine, layer, depth):
    shift = (layer.astype(F32) - (depth - 1) / 2.0) * sine
    lower = jnp.floor(shift)
    copies = apart.shape[0] // sine.shape[0]

    def filled(value):
        return jnp.concatenate([value.astype(BF)] * copies, axis=0)

    def weight(offset):
        return filled(jnp.maximum(0.0, 1.0 - jnp.abs(offset - shift)))

    beyond = jnp.where(
        apart == filled(lower + 1.0), weight(lower + 1.0), jnp.zeros(apart.shape, BF)
    )
    return jnp.where(apart == filled(lower), weight(lower), beyond)


def slots_of_items(row_ref, strip_rows, capacity):
    tilts, boxes = row_ref.shape
    strips = [quotient(row_ref[t, b], strip_rows) for t in range(tilts) for b in range(boxes)]
    slots = []
    for n, strip in enumerate(strips):
        place = strip * capacity
        for other in strips[:n]:
            place = place + jnp.where(other == strip, 1, 0)
        slots.append(place)
    return strips, slots


def splat_rows(values, rows, width):
    row_at = lax.broadcasted_iota(jnp.int32, (rows, width), 0)
    block = jnp.zeros((rows, width), F32)
    for i, value in enumerate(values):
        block = jnp.where(row_at == i, value.astype(F32), block)
    return block.astype(BF)


def project_kernel(
    row_ref, angle_ref, vol_ref, *refs, depth, tilts, groups, ks, first, strip_rows, capacity
):
    outs, (total, sines) = refs[: len(ks)], refs[-2:]
    step = pl.program_id(0)
    me = lax.axis_index("tilt")
    if first:
        lhs, wide = refs[len(ks)], refs[len(ks) + 1]
        rows, layers, width = vol_ref.shape
        wide[...] = vol_ref[...].reshape(rows * layers, width).astype(F32)
        for z in range(layers):
            lhs[:, z * width : (z + 1) * width] = wide[pl.ds(z, rows, stride=layers), :].astype(BF)
    else:
        lhs = vol_ref
        rows = lhs.shape[0]
        width = outs[0].shape[1]
        layers = lhs.shape[1] // width

    @pl.when(step == 0)
    def _():
        total[...] = jnp.zeros_like(total)
        note_sines(angle_ref, sines)

    apart = iota_apart((width, width), 1, 0)

    def block(k, z, t):
        sine = sines[lax.rem(me + k, groups) * tilts + t]
        return tap_block(apart, sine, step * layers + z, depth)

    for z in range(0, layers, 2):
        for i, k in enumerate(ks):
            table = jnp.concatenate(
                [
                    jnp.concatenate([block(k, z + half, t) for t in range(tilts)], axis=1)
                    for half in range(2)
                ],
                axis=0,
            )
            span = slice(i * tilts * width, (i + 1) * tilts * width)
            total[:, span] += jnp.dot(
                lhs[:, z * width : (z + 2) * width], table, preferred_element_type=F32
            )

    @pl.when(step == pl.num_programs(0) - 1)
    def _():
        _, slots = slots_of_items(row_ref, strip_rows, capacity)
        meta = splat_rows(slots, outs[0].shape[0] - tilts * rows, width)
        for i in range(len(ks)):
            for t in range(tilts):
                start = (i * tilts + t) * width
                outs[i][t * rows : (t + 1) * rows, :] = total[:, start : start + width].astype(BF)
            outs[i][tilts * rows :, :] = meta


def project(volume, rows_of, angles, tilts, groups, ks, first, depth, width, strip_rows, capacity):
    rows = volume.shape[0]
    layers = min(16, depth)
    length = tilts * rows + -(-tilts * rows_of.shape[1] // 16) * 16
    scalars = pl.BlockSpec(memory_space=pltpu.SMEM)
    flat = pl.BlockSpec((rows, layers * width), lambda i: (0, i))
    source = pl.BlockSpec((rows, layers, width), lambda i: (0, i, 0)) if first else flat
    return pl.pallas_call(
        functools.partial(
            project_kernel,
            depth=depth,
            tilts=tilts,
            groups=groups,
            ks=ks,
            first=first,
            strip_rows=strip_rows,
            capacity=capacity,
        ),
        out_shape=[jax.ShapeDtypeStruct((length, width), BF)] * len(ks)
        + ([jax.ShapeDtypeStruct((rows, depth * width), BF)] if first else []),
        grid=(depth // layers,),
        in_specs=[scalars] * 2 + [source],
        out_specs=[pl.BlockSpec((length, width), lambda i: (0, 0))] * len(ks)
        + ([flat] if first else []),
        scratch_shapes=([pltpu.VMEM((rows * layers, width), F32)] if first else [])
        + [
            pltpu.VMEM((rows, len(ks) * tilts * width), F32),
            pltpu.VMEM((groups * tilts, 16, width), F32),
        ],
        compiler_params=GRANT,
        name="project_first" if first else "project_rest",
    )(rows_of, angles, volume)


def back_kernel(
    angle_ref, cut_ref, *refs, depth, tilts, boxes, groups, scale
):
    metas, (out_ref, lhs, sines) = refs[:groups], refs[groups:]
    step = pl.program_id(0)
    me = lax.axis_index("tilt")
    rows, layers, width = out_ref.shape
    slab_rows, length = rows // boxes, cut_ref.shape[1]
    apart = iota_apart((width, width), 0, 1)

    @pl.when(step == 0)
    def _():
        note_sines(angle_ref, sines)
        ahead = lax.broadcasted_iota(jnp.int32, (slab_rows, length), 1)
        ahead = (ahead - lax.broadcasted_iota(jnp.int32, (slab_rows, length), 0)).astype(F32)
        for k in range(groups):
            group = lax.rem(me + groups - k, groups)
            for t in range(tilts):
                picks = []
                for b in range(boxes):
                    slot = metas[k][t * boxes + b : t * boxes + b + 1, :1].astype(F32)
                    picks.append(ones_where(ahead == slot * float(slab_rows)))
                start = (k * tilts + t) * width
                lhs[:, start : start + width] = jnp.dot(
                    jnp.concatenate(picks, axis=0), cut_ref[group], preferred_element_type=F32
                ).astype(BF)

    def block(k, t, z):
        sine = sines[lax.rem(me + groups - k, groups) * tilts + t]
        return tap_block(apart, sine, step * layers + z, depth)

    flat = out_ref.reshape(rows * layers, width)
    for z in range(0, layers, 2):
        table = jnp.concatenate(
            [
                jnp.concatenate([block(k, t, z + half) for half in range(2)], axis=1)
                for k in range(groups)
                for t in range(tilts)
            ],
            axis=0,
        )
        result = jnp.dot(lhs[...], table, preferred_element_type=F32) * scale
        for half in range(2):
            flat[pl.ds(z + half, rows, stride=layers), :] = result[
                :, half * width : (half + 1) * width
            ]


def back_project(cuts, slabs, angles, boxes, tilts, rows, depth, scale):
    groups, _, width = cuts.shape
    layers = min(8, depth)
    meta = slabs[0].shape[0] - tilts * rows
    at = tilts * rows // meta
    scalars = pl.BlockSpec(memory_space=pltpu.SMEM)
    return pl.pallas_call(
        functools.partial(
            back_kernel, depth=depth, tilts=tilts, boxes=boxes, groups=groups, scale=scale
        ),
        out_shape=jax.ShapeDtypeStruct((rows, depth, width), F32),
        grid=(depth // layers,),
        in_specs=[scalars]
        + [pl.BlockSpec(cuts.shape, lambda i: (0, 0, 0))]
        + [pl.BlockSpec((meta, width), lambda i: (at, 0))] * groups,
        out_specs=pl.BlockSpec((rows, layers, width), lambda i: (0, i, 0)),
        scratch_shapes=[
            pltpu.VMEM((rows, groups * tilts * width), BF),
            pltpu.VMEM((groups * tilts, 16, width), F32),
        ],
        compiler_params=GRANT,
        name="back_project",
    )(angles, cuts, *slabs)


def pack_kernel(row_ref, col_ref, *refs, groups, tile_count, strip_rows, capacity, slab_rows):
    slabs, outs = refs[:groups], refs[groups : groups + tile_count]
    item_ref, within_ref, left_ref = refs[groups + tile_count :]
    _, boxes = row_ref.shape
    width = slabs[0].shape[1]
    height = slab_rows * groups
    my_tilt, my_tile = lax.axis_index("tilt"), lax.axis_index("tile")
    strips, slots = slots_of_items(row_ref, strip_rows, capacity)
    margin = 2 * capacity

    def clear(i, carry):
        item_ref[i] = -1
        within_ref[i] = ABSENT
        left_ref[i] = 0
        return carry

    lax.fori_loop(0, tile_count * capacity + 2 * margin, clear, 0)
    for n, (strip, slot) in enumerate(zip(strips, slots, strict=True)):
        t, b = n // boxes, n % boxes
        item_ref[slot + margin] = n
        within_ref[slot + margin] = row_ref[t, b] - strip * strip_rows + t * strip_rows
        left_ref[slot + margin] = col_ref[t, b]
    sources = [lax.rem(my_tilt + groups - k, groups) for k in range(groups)]

    def slab_of(k, item, begin, size):
        start = pl.multiple_of(jnp.maximum(item, 0) * slab_rows + begin, 16)
        block = slabs[k][pl.ds(start, size), :]
        return jnp.where(item >= 0, block, jnp.zeros_like(block))

    for d in range(tile_count):
        out = outs[d]
        strip = lax.rem(my_tile + d, tile_count)
        metas = []

        def item_at(offset, r):
            spot = (strip + offset + 2) * capacity + r
            metas.append(within_ref[spot])
            metas.append(left_ref[spot])
            return item_ref[spot]

        for r in range(capacity):
            item = item_at(0, r)
            for k in range(groups):
                begin = pl.multiple_of(r * height + sources[k] * slab_rows, slab_rows)
                out[pl.ds(begin, slab_rows), :] = slab_of(k, item, 0, slab_rows)
        base = capacity * height
        for offset, wanted, begin in ((2, 0, 0), (-2, groups - 1, slab_rows - REACH)):
            for r in range(capacity):
                item = item_at(offset, r)
                block = slab_of(0, item, begin, REACH)
                for k in range(1, groups):
                    block = jnp.where(sources[k] == wanted, slab_of(k, item, begin, REACH), block)
                out[base : base + REACH, :] = block
                base += REACH
        out[base:, :] = splat_rows(metas, out.shape[0] - base, width)


def pack(slabs, rows_of, cols_of, slab_rows, tile_count, strip_rows, capacity):
    groups = len(slabs)
    width = slabs[0].shape[1]
    meta_rows = -(-6 * capacity // 16) * 16
    length = capacity * (slab_rows * groups + 2 * REACH) + meta_rows
    slots = (tile_count + 4) * capacity
    return pl.pallas_call(
        functools.partial(
            pack_kernel,
            groups=groups,
            tile_count=tile_count,
            strip_rows=strip_rows,
            capacity=capacity,
            slab_rows=slab_rows,
        ),
        out_shape=[jax.ShapeDtypeStruct((length, width), BF)] * tile_count,
        in_specs=[pl.BlockSpec(memory_space=pltpu.SMEM)] * 2
        + [pl.BlockSpec(memory_space=pltpu.VMEM)] * groups,
        out_specs=[pl.BlockSpec(memory_space=pltpu.VMEM)] * tile_count,
        scratch_shapes=[pltpu.SMEM((slots,), jnp.int32)] * 3,
        compiler_params=GRANT,
        name="pack",
    )(rows_of, cols_of, slabs[0], *[near(slab) for slab in slabs[1:]])


def hi_lo(block):
    high = block.astype(BF)
    return high, (block - high.astype(F32)).astype(BF)


def place_kernel(measured_ref, after_ref, *refs, tilts, strip_rows, height, capacity, tile_count):
    parcels = refs[:tile_count]
    canvas_ref, next_ref, prev_ref, placed, onehot = refs[tile_count:]
    _, width = parcels[0].shape
    rows, image_width = canvas_ref.shape[1:]
    column = iota_apart((width, image_width), 1, 0)
    apart = iota_apart((rows, height), 0, 1)
    edge_apart = iota_apart((REACH, REACH), 0, 1)
    base = capacity * height
    meta = base + 2 * capacity * REACH

    def spread_out(parcel, begin, size, q):
        left = parcel[meta + 2 * q + 1 : meta + 2 * q + 2, :1]
        picks = ones_where(column == left)
        return jnp.dot(parcel[begin : begin + size, :], picks, preferred_element_type=F32).astype(BF)

    def row_of(parcel, q, t):
        own = parcel[meta + 2 * q : meta + 2 * q + 1, :].astype(F32) - float(t * strip_rows)
        return jnp.where((own >= 0) & (own < strip_rows), own, float(ABSENT))

    index = 0
    for parcel in parcels:
        for r in range(capacity):
            placed[index * height : (index + 1) * height, :] = spread_out(parcel, r * height, height, r)
            for t in range(tilts):
                target = (row_of(parcel, r, t) + float(REACH)).astype(BF)
                onehot[t * rows : (t + 1) * rows, index * height : (index + 1) * height] = (
                    ones_where(apart == target)
                )
            index += 1
    total = jnp.dot(onehot[...], placed[...], preferred_element_type=F32)
    for t in range(tilts):
        canvas_ref[t] = total[t * rows : (t + 1) * rows]
    for side in range(2):
        blocks = [[] for _ in range(tilts)]
        values = []
        for parcel in parcels:
            for r in range(capacity):
                q = (1 + side) * capacity + r
                begin = base + side * capacity * REACH + r * REACH
                values.append(spread_out(parcel, begin, REACH, q))
                for t in range(tilts):
                    target = row_of(parcel, q, t)[:, :REACH]
                    if side == 1:
                        target = target + float(height - 2 * strip_rows)
                    blocks[t].append(ones_where(edge_apart == target.astype(BF)))
        tall = jnp.concatenate(values, axis=0)
        for t in range(tilts):
            picks = jnp.concatenate(blocks[t], axis=1)
            edge = jnp.dot(picks, tall, preferred_element_type=F32)
            begin = rows - REACH if side == 0 else 0
            canvas_ref[t, begin : begin + REACH, :] = edge
    reach = strip_rows + REACH
    for t in range(tilts):
        next_ref[t, :reach, :] = canvas_ref[t, strip_rows : strip_rows + reach, :].astype(BF)
        prev_ref[t, :reach, :] = canvas_ref[t, REACH : REACH + reach, :].astype(BF)
        high, low = hi_lo(measured_ref[t, strip_rows - HR :, :])
        next_ref[t, reach:, :] = jnp.concatenate([high, low], axis=0)
        high, low = hi_lo(after_ref[t, :HR, :])
        prev_ref[t, reach:, :] = jnp.concatenate([high, low], axis=0)


def place(measured, after, parcels, height, capacity):
    tilts, strip_rows, image_width = measured.shape
    tile_count = len(parcels)
    rows = 2 * strip_rows + 2 * REACH
    halo = strip_rows + REACH + 2 * HR
    whole = pl.BlockSpec(memory_space=pltpu.VMEM)
    return pl.pallas_call(
        functools.partial(
            place_kernel,
            tilts=tilts,
            strip_rows=strip_rows,
            height=height,
            capacity=capacity,
            tile_count=tile_count,
        ),
        out_shape=[
            jax.ShapeDtypeStruct((tilts, rows, image_width), F32),
            jax.ShapeDtypeStruct((tilts, halo, image_width), BF),
            jax.ShapeDtypeStruct((tilts, halo, image_width), BF),
        ],
        in_specs=[whole] * (2 + tile_count),
        out_specs=[whole] * 3,
        scratch_shapes=[
            pltpu.VMEM((tile_count * capacity * height, image_width), BF),
            pltpu.VMEM((tilts * rows, tile_count * capacity * height), BF),
        ],
        compiler_params=GRANT,
        name="place",
    )(measured, near(after), parcels[0], *[near(p) for p in parcels[1:]])


def transfer_kernel(defocus_ref, out_ref):
    tilts, _, image_width, _ = out_ref.shape
    lanes = 128
    row = lax.broadcasted_iota(jnp.int32, (8, lanes), 0)
    lane = lax.broadcasted_iota(jnp.int32, (8, lanes), 1)
    down = lax.broadcasted_iota(jnp.int32, (8, lanes), 0)
    for t in range(tilts):
        for i in range(HR + 1):
            rho_sq = (i * i + lane * lane).astype(F32)
            value = jnp.exp(-rho_sq / (2.0 * HR * HR)) * jnp.cos(defocus_ref[t] * rho_sq) / float(HR * HR)
            value = jnp.where(lane <= HR, value, 0.0)
            for begin in range(0, image_width, 16):
                for column in range(0, image_width, lanes):
                    if begin - column > lanes + HR or column - begin > 16 + HR:
                        out_ref[t, i, begin : begin + 16, column : column + lanes] = jnp.zeros(
                            (16, lanes), BF
                        )
                        continue
                    parts = []
                    for half in range(2):
                        apart = jnp.abs(down + (begin + 8 * half - column) - lane)
                        parts.append(
                            jnp.take_along_axis(value, jnp.minimum(apart, lanes - 1), axis=1)
                        )
                    out_ref[t, i, begin : begin + 16, column : column + lanes] = jnp.concatenate(
                        parts, axis=0
                    ).astype(BF)


def transfer_tables(defocus, image_width):
    return pl.pallas_call(
        transfer_kernel,
        out_shape=jax.ShapeDtypeStruct((defocus.shape[0], HR + 1, image_width, image_width), BF),
        in_specs=[pl.BlockSpec(memory_space=pltpu.SMEM)],
        out_specs=pl.BlockSpec(memory_space=pltpu.VMEM),
        compiler_params=GRANT,
        name="transfer",
    )(defocus)


def convolve(source, parts, table_ref, t, height):
    rows = source.shape[0]
    for i in range(HR + 1):
        parts[i, :rows, :] = jnp.dot(source, table_ref[t, i], preferred_element_type=F32)
    total = parts[0, HR : HR + height, :]
    for i in range(1, HR + 1):
        total = total + (
            parts[i, HR + i : HR + i + height, :] + parts[i, HR - i : HR - i + height, :]
        )
    return total


def filter_kernel(
    canvas_ref, above_ref, below_ref, measured_ref, after_ref, table_ref, *refs, height, capacity
):
    tile_count = len(refs) - 4
    parcels, (residual_ref, out_ref, parts, back) = refs[:tile_count], refs[tile_count:]
    groups = out_ref.shape[0]
    slab_rows = height // groups
    tilts, strip_rows, image_width = measured_ref.shape
    rows = canvas_ref.shape[1]
    my_tile = lax.axis_index("tile")
    first = my_tile * strip_rows
    image_rows = tile_count * strip_rows
    reach = strip_rows + REACH

    def inside(count, start):
        at = lax.broadcasted_iota(jnp.int32, (count, image_width), 0) + (first + start)
        return (at >= 0) & (at < image_rows)

    at_top, at_end = my_tile == 0, my_tile == tile_count - 1
    for t in range(tilts):
        upper = jnp.where(at_top, 0.0, above_ref[t, :reach, :].astype(F32))
        lower = jnp.where(at_end, 0.0, below_ref[t, :reach, :].astype(F32))
        field = canvas_ref[t] + jnp.concatenate([upper, lower], axis=0)
        field = jnp.where(inside(rows, -REACH), field, 0.0)
        known = jnp.concatenate(
            [
                above_ref[t, reach : reach + HR, :].astype(F32)
                + above_ref[t, reach + HR :, :].astype(F32),
                measured_ref[t],
                after_ref[t],
                below_ref[t, reach : reach + HR, :].astype(F32)
                + below_ref[t, reach + HR :, :].astype(F32),
            ],
            axis=0,
        )
        count = rows - 2 * HR
        rest = known - convolve(field.astype(BF), parts, table_ref, t, count)
        residual_ref[t] = rest[HR : HR + strip_rows]
        rest = jnp.where(inside(count, -HR), rest, 0.0)
        count -= 2 * HR
        image = convolve(rest.astype(BF), parts, table_ref, t, count)
        back[t * count : (t + 1) * count, :] = jnp.where(inside(count, 0), image, 0.0).astype(BF)
    width = parcels[0].shape[1]
    count = 2 * strip_rows
    apart = iota_apart((height, count), 1, 0)
    column = iota_apart((image_width, width), 0, 1)
    meta = capacity * (height + 2 * REACH)
    for d, parcel in enumerate(parcels):
        sender = lax.rem(my_tile + tile_count - d, tile_count)
        for r in range(capacity):
            top = parcel[meta + 2 * r : meta + 2 * r + 1, :].astype(F32)
            picks = []
            for t in range(tilts):
                own = top - float(t * strip_rows)
                own = jnp.where((own >= 0) & (own < strip_rows), own, float(ABSENT)).astype(BF)
                picks.append(ones_where(apart == own[:, :1]))
            cut = jnp.dot(
                jnp.concatenate(picks, axis=1), back[...], preferred_element_type=F32
            ).astype(BF)
            left = parcel[meta + 2 * r + 1 : meta + 2 * r + 2, :]
            columns = ones_where(column == left)
            window = jnp.dot(cut, columns, preferred_element_type=F32).astype(BF)
            for i in range(groups):
                out_ref[i, sender, r * slab_rows : (r + 1) * slab_rows, :] = window[
                    i * slab_rows : (i + 1) * slab_rows
                ]


def filter_and_cut(canvas, above, below, measured, after, table, parcels, height, capacity, groups):
    tilts, strip_rows, image_width = measured.shape
    tile_count = len(parcels)
    width = parcels[0].shape[1]
    rows = canvas.shape[1]
    whole = pl.BlockSpec(memory_space=pltpu.VMEM)
    slots = (groups, tile_count, capacity * height // groups, width)
    return pl.pallas_call(
        functools.partial(filter_kernel, height=height, capacity=capacity),
        out_shape=[jax.ShapeDtypeStruct(measured.shape, F32), jax.ShapeDtypeStruct(slots, BF)],
        in_specs=[whole] * (6 + tile_count),
        out_specs=[whole] * 2,
        scratch_shapes=[
            pltpu.VMEM((HR + 1, rows, image_width), F32),
            pltpu.VMEM((tilts * 2 * strip_rows, image_width), BF),
        ],
        compiler_params=GRANT,
        name="filter_and_cut",
    )(near(canvas), near(above), near(below), measured, near(after), near(table), parcels[0], *[near(p) for p in parcels[1:]])


def shards(volumes, angles, defocus, row_offsets, col_offsets, measured):
    boxes, slab_rows, depth, width = volumes.shape
    tilts, strip_rows, image_width = measured.shape
    tile_count, groups = lax.axis_size("tile"), lax.axis_size("tilt")
    height, rows = slab_rows * groups, boxes * slab_rows
    capacity = max(2, -(-boxes * tilts // tile_count))
    assert tilts * strip_rows <= 256 and tile_count * capacity <= 256
    rows_of, cols_of = row_offsets.T, col_offsets.T
    after = ring(measured, "tile", -1)
    kernel = transfer_tables(defocus, image_width)
    slabs = [None] * groups
    volume = volumes.reshape(rows, depth, width)
    half = groups // 2 + 1
    early, late = tuple(range(1, half)), (*range(half, groups), 0)
    sizes = (depth, width, strip_rows, capacity)
    *parts, flat = project(volume, rows_of, angles, tilts, groups, early, True, *sizes)
    for k, part in zip(early, parts, strict=True):
        slabs[k] = ring(part, "tilt", k)
    parts = project(flat, rows_of, angles, tilts, groups, late, False, *sizes)
    for k, part in zip(late, parts, strict=True):
        slabs[k] = ring(part, "tilt", k) if k else part
    parcels = pack(slabs, rows_of, cols_of, slab_rows, tile_count, strip_rows, capacity)
    parcels = [p if d == 0 else ring(p, "tile", d) for d, p in enumerate(parcels)]
    canvas, onward, backward = place(measured, after, parcels, height, capacity)
    above, below = ring(onward, "tile", 1), ring(backward, "tile", -1)
    residual, cuts = filter_and_cut(
        canvas, above, below, measured, after, kernel, parcels, height, capacity, groups
    )
    cuts = cuts.reshape(groups * tile_count, capacity * slab_rows, width)
    cuts = lax.all_to_all(cuts, ("tilt", "tile"), split_axis=0, concat_axis=0, tiled=True)
    cuts = cuts.reshape(groups, tile_count * capacity * slab_rows, width)
    step = back_project(cuts, slabs, angles, boxes, tilts, rows, depth, 1.0 / (tilts * groups))
    return residual, step.reshape(boxes, slab_rows, depth, width)


def solution(mesh):
    in_specs = (
        P("tile", "tilt", None, None),
        P(),
        P("tilt"),
        P("tile", "tilt"),
        P("tile", "tilt"),
        P("tilt", "tile", None),
    )
    out_specs = (P("tilt", "tile", None), P("tile", "tilt", None, None))

    return jax.shard_map(shards, mesh=mesh, in_specs=in_specs, out_specs=out_specs, check_vma=False)
```

profile of v0, /device:TPU:0, one launch (start us, length us, event | category | flops | bytes accessed | tf_op | source)
XLA Modules:
  0.0 85.4 jit_solution(6201267126359567506)
XLA Ops:
  0.6 0.0 copy-start
  0.6 1.9 %copy-done = bf16[6,32,64,128]{3,2,1,0:T(8,128)(2,1)S(1)} copy-done((bf16[6,32,64,128]{3,2,1,0:T(8,128)(2,1)S(1)}, bf16[6,32,64,128]{3,2,1,0:T(8,128)(2,1)}, u32[]{:S(2)}) %copy-start) | copy-done | bytes 3145752
  2.5 0.0 copy-start.2
  2.5 0.7 copy-done.2
  3.2 0.0 copy-start.3
  3.2 0.7 copy-done.3
  3.9 0.0 copy-start.1
  3.9 0.0 copy-start.5
  3.9 7.5 %project_first.1 = (bf16[400,128]{1,0:T(8,128)(2,1)S(1)}, bf16[400,128]{1,0:T(8,128)(2,1)S(1)}, bf16[192,8192]{1,0:T(8,128)(2,1)S(1)}) custom-call(s32[2,6]{1,0:T(2,128)S(1)} %bitcast.9, f32[8]{0:T(128)S(1)} %copy-done.3, bf16[192,64,128]{2,1,0:T(8,128)(2,1)S(1)} %bitcast.6), custom_call_target="tpu_custom_call" | custom-call | tf_op jit(solution)/shard_map/project_first/pallas_call | solution.py:146
  11.4 0.0 copy-start.6
  11.4 4.3 %project_rest.1 = (bf16[400,128]{1,0:T(8,128)(2,1)S(1)}, bf16[400,128]{1,0:T(8,128)(2,1)S(1)}) custom-call(s32[2,6]{1,0:T(2,128)S(1)} %bitcast.10, f32[8]{0:T(128)S(1)} %copy-done.3, bf16[192,8192]{1,0:T(8,128)(2,1)S(1)} %get-tuple-element.20.vol_ref), custom_call_target="tpu_custom_call" | custom-call | tf_op jit(solution)/shard_map/project_rest/pallas_call | solution.py:146
  15.7 5.2 %collective-permute-start.3 = (bf16[400,128]{1,0:T(8,128)(2,1)S(1)}, bf16[400,128]{1,0:T(8,128)(2,1)S(1)}, u32[]{:S(2)}, u32[]{:S(2)}) collective-permute-start(bf16[400,128]{1,0:T(8,128)(2,1)S(1)} %get-tuple-element.24), channel_id=1, source_target_pairs={{0,24},{8,0},{16,8},{24,16},{1,25},{9,1},{17,9},{25,17},{2,26},{10... | collective-permute-start | bytes 307208 | tf_op jit(solution)/shard_map/ppermute | solution.py:20
  20.9 0.0 collective-permute-start.1
  20.9 1.0 %collective-permute-start.2 = (bf16[400,128]{1,0:T(8,128)(2,1)S(1)}, bf16[400,128]{1,0:T(8,128)(2,1)S(1)}, u32[]{:S(2)}, u32[]{:S(2)}) collective-permute-start(bf16[400,128]{1,0:T(8,128)(2,1)S(1)} %get-tuple-element.23), channel_id=1, source_target_pairs={{0,16},{8,24},{16,0},{24,8},{1,17},{9,25},{17,1},{25,9},{2,18},{10... | collective-permute-start | bytes 307208 | tf_op jit(solution)/shard_map/ppermute | solution.py:20
  21.8 0.0 copy-done.1
  21.8 1.0 %collective-permute-start = (f32[2,128,256]{2,1,0:T(8,128)S(1)}, f32[2,128,256]{2,1,0:T(8,128)S(1)}, u32[]{:S(2)}, u32[]{:S(2)}) collective-permute-start(f32[2,128,256]{2,1,0:T(8,128)S(1)} %copy-done.1), channel_id=1, source_target_pairs={{0,7},{1,0},{2,1},{3,2},{4,3},{5,4},{6,5},{7,6},{8,15},{9,8},{10,9... | collective-permute-start | bytes 786440 | tf_op jit(solution)/shard_map/ppermute | solution.py:20
  22.9 1.2 %collective-permute-done.3.refs_3_ = bf16[400,128]{1,0:T(8,128)(2,1)S(1)} collective-permute-done((bf16[400,128]{1,0:T(8,128)(2,1)S(1)}, bf16[400,128]{1,0:T(8,128)(2,1)S(1)}, u32[]{:S(2)}, u32[]{:S(2)}) %collective-permute-start.3) | collective-permute-done | bytes 102432 | tf_op jit(solution)/shard_map/ppermute | solution.py:20
  24.1 4.1 %collective-permute-done.1.refs_1_ = bf16[400,128]{1,0:T(8,128)(2,1)S(1)} collective-permute-done((bf16[400,128]{1,0:T(8,128)(2,1)S(1)}, bf16[400,128]{1,0:T(8,128)(2,1)S(1)}, u32[]{:S(2)}, u32[]{:S(2)}) %collective-permute-start.1) | collective-permute-done | bytes 102432 | tf_op jit(solution)/shard_map/ppermute | solution.py:20
  28.2 2.3 %collective-permute-done.2.refs_2_ = bf16[400,128]{1,0:T(8,128)(2,1)S(1)} collective-permute-done((bf16[400,128]{1,0:T(8,128)(2,1)S(1)}, bf16[400,128]{1,0:T(8,128)(2,1)S(1)}, u32[]{:S(2)}, u32[]{:S(2)}) %collective-permute-start.2) | collective-permute-done | bytes 102432 | tf_op jit(solution)/shard_map/ppermute | solution.py:20
  30.5 0.0 copy-done.5
  30.5 1.3 %pack.1 = (bf16[336,128]{1,0:T(8,128)(2,1)S(1)}, bf16[336,128]{1,0:T(8,128)(2,1)S(1)}, bf16[336,128]{1,0:T(8,128)(2,1)S(1)}, bf16[336,128]{1,0:T(8,128)(2,1)S(1)...) custom-call(s32[2,6]{1,0:T(2,128)S(1)} %bitcast.11, ...), custom_call_target="tpu_custom_call" | custom-call | tf_op jit(solution)/shard_map/pack/pallas_call | solution.py:309
  31.8 0.1 collective-permute-start.4
  31.9 1.6 %collective-permute-start.5 = (bf16[336,128]{1,0:T(8,128)(2,1)S(1)}, bf16[336,128]{1,0:T(8,128)(2,1)S(1)}, u32[]{:S(2)}, u32[]{:S(2)}) collective-permute-start(bf16[336,128]{1,0:T(8,128)(2,1)S(1)} %get-tuple-element.27), channel_id=1, source_target_pairs={{0,2},{1,3},{2,4},{3,5},{4,6},{5,7},{6,0},{7,1},{8,10},{9,11},{10,... | collective-permute-start | bytes 258056 | tf_op jit(solution)/shard_map/ppermute | solution.py:20
  33.4 2.3 %collective-permute-start.6 = (bf16[336,128]{1,0:T(8,128)(2,1)S(1)}, bf16[336,128]{1,0:T(8,128)(2,1)S(1)}, u32[]{:S(2)}, u32[]{:S(2)}) collective-permute-start(bf16[336,128]{1,0:T(8,128)(2,1)S(1)} %get-tuple-element.28), channel_id=1, source_target_pairs={{0,3},{1,4},{2,5},{3,6},{4,7},{5,0},{6,1},{7,2},{8,11},{9,12},{10,... | collective-permute-start | bytes 258056 | tf_op jit(solution)/shard_map/ppermute | solution.py:20
  35.7 0.5 collective-permute-start.7
  36.3 0.7 collective-permute-done.4.refs_1_
  37.0 0.0 collective-permute-start.8
  37.0 1.3 %collective-permute-done.5.refs_2_ = bf16[336,128]{1,0:T(8,128)(2,1)S(1)} collective-permute-done((bf16[336,128]{1,0:T(8,128)(2,1)S(1)}, bf16[336,128]{1,0:T(8,128)(2,1)S(1)}, u32[]{:S(2)}, u32[]{:S(2)}) %collective-permute-start.5) | collective-permute-done | bytes 86048 | tf_op jit(solution)/shard_map/ppermute | solution.py:20
  38.3 1.4 %collective-permute-start.9 = (bf16[336,128]{1,0:T(8,128)(2,1)S(1)}, bf16[336,128]{1,0:T(8,128)(2,1)S(1)}, u32[]{:S(2)}, u32[]{:S(2)}) collective-permute-start(bf16[336,128]{1,0:T(8,128)(2,1)S(1)} %get-tuple-element.31), channel_id=1, source_target_pairs={{0,6},{1,7},{2,0},{3,1},{4,2},{5,3},{6,4},{7,5},{8,14},{9,15},{10,... | collective-permute-start | bytes 258056 | tf_op jit(solution)/shard_map/ppermute | solution.py:20
  39.8 1.3 %collective-permute-done.6.refs_3_ = bf16[336,128]{1,0:T(8,128)(2,1)S(1)} collective-permute-done((bf16[336,128]{1,0:T(8,128)(2,1)S(1)}, bf16[336,128]{1,0:T(8,128)(2,1)S(1)}, u32[]{:S(2)}, u32[]{:S(2)}) %collective-permute-start.6) | collective-permute-done | bytes 86048 | tf_op jit(solution)/shard_map/ppermute | solution.py:20
  41.0 0.0 collective-permute-start.10
  41.0 0.5 collective-permute-done.7.refs_4_
  41.5 0.7 collective-permute-done.8.refs_5_
  42.2 0.9 %collective-permute-done.9.refs_6_ = bf16[336,128]{1,0:T(8,128)(2,1)S(1)} collective-permute-done((bf16[336,128]{1,0:T(8,128)(2,1)S(1)}, bf16[336,128]{1,0:T(8,128)(2,1)S(1)}, u32[]{:S(2)}, u32[]{:S(2)}) %collective-permute-start.9) | collective-permute-done | bytes 86048 | tf_op jit(solution)/shard_map/ppermute | solution.py:20
  43.0 0.1 collective-permute-done.10.refs_7_
  43.1 0.0 collective-permute-done.after_ref
  43.1 1.7 %place.1 = (f32[2,288,256]{2,1,0:T(8,128)S(1)}, bf16[2,160,256]{2,1,0:T(8,128)(2,1)S(1)}, bf16[2,160,256]{2,1,0:T(8,128)(2,1)S(1)}) custom-call(f32[2,128,256]{2,1,0:T(8,128)S(1)} %copy-done.1, f32[2,128,256]{2,1,0:T(8,128)S(1)} %collective-permute-done.after_ref, bf16[336,128]{1,0:T(8,128)(2,1)S(1)} %get-tuple-element.25.refs_0_, ...), custom_call_target="tpu_custom_call" | custom-call | tf_op jit(solution)/shard_map/place/pallas_call | solution.py:401
  44.9 1.1 %collective-permute-start.11 = (bf16[2,160,256]{2,1,0:T(8,128)(2,1)S(1)}, bf16[2,160,256]{2,1,0:T(8,128)(2,1)S(1)}, u32[]{:S(2)}, u32[]{:S(2)}) collective-permute-start(bf16[2,160,256]{2,1,0:T(8,128)(2,1)S(1)} %get-tuple-element.34), channel_id=1, source_target_pairs={{0,1},{1,2},{2,3},{3,4},{4,5},{5,6},{6,7},{7,0},{8,9},{9,10},{10,1... | collective-permute-start | bytes 491528 | tf_op jit(solution)/shard_map/ppermute | solution.py:20
  46.0 1.6 %collective-permute-start.12 = (bf16[2,160,256]{2,1,0:T(8,128)(2,1)S(1)}, bf16[2,160,256]{2,1,0:T(8,128)(2,1)S(1)}, u32[]{:S(2)}, u32[]{:S(2)}) collective-permute-start(bf16[2,160,256]{2,1,0:T(8,128)(2,1)S(1)} %get-tuple-element.35), channel_id=1, source_target_pairs={{0,7},{1,0},{2,1},{3,2},{4,3},{5,4},{6,5},{7,6},{8,15},{9,8},{10,9... | collective-permute-start | bytes 491528 | tf_op jit(solution)/shard_map/ppermute | solution.py:20
  47.6 0.0 copy-done.6
  47.6 1.3 %transfer.1.table_ref = bf16[2,9,256,256]{3,2,1,0:T(8,128)(2,1)S(1)} custom-call(f32[2]{0:T(128)S(1)} %copy-done.6), custom_call_target="tpu_custom_call" | custom-call | tf_op jit(solution)/shard_map/transfer/pallas_call | solution.py:456
  48.9 0.0 copy-start.4
  48.9 1.7 %collective-permute-done.11.above_ref = bf16[2,160,256]{2,1,0:T(8,128)(2,1)S(1)} collective-permute-done((bf16[2,160,256]{2,1,0:T(8,128)(2,1)S(1)}, bf16[2,160,256]{2,1,0:T(8,128)(2,1)S(1)}, u32[]{:S(2)}, u32[]{:S(2)}) %collective-permute-start.11) | collective-permute-done | bytes 163872 | tf_op jit(solution)/shard_map/ppermute | solution.py:20
  50.7 0.0 collective-permute-done.12.below_ref
  50.7 5.7 %filter_and_cut.1 = (f32[2,128,256]{2,1,0:T(8,128)}, bf16[4,8,64,128]{3,2,1,0:T(8,128)(2,1)S(1)}) custom-call(f32[2,288,256]{2,1,0:T(8,128)S(1)} %get-tuple-element.33.canvas_ref, bf16[2,160,256]{2,1,0:T(8,128)(2,1)S(1)} %collective-permute-done.11.above_ref, bf16[2,160,256]{2,1,0:T(8,128)(2,1)S(1)} %collective-permute-done.12.below_ref, ...), custom_call_target="tpu_custom_call" | custom-call | tf_op jit(solution)/shard_map/filter_and_cut/pallas_call | solution.py:553
  56.3 19.9 %all_to_all.5 = bf16[32,64,128]{2,1,0:T(8,128)(2,1)S(1)} all-to-all(bf16[32,64,128]{2,1,0:T(8,128)(2,1)S(1)} %bitcast.8), channel_id=1, replica_groups=mesh['tilt'=4,'tile'=8] {'tilt','tile'}, dimensions={0} | all-to-all | bytes 1048576 | tf_op jit(solution)/shard_map/all_to_all | solution.py:596
  76.2 0.0 copy-done.4
  76.2 9.1 %back_project.1 = f32[192,64,128]{2,1,0:T(8,128)} custom-call(f32[8]{0:T(128)S(1)} %copy-done.4, bf16[4,512,128]{2,1,0:T(8,128)(2,1)S(1)} %bitcast.7, bf16[400,128]{1,0:T(8,128)(2,1)S(1)} %get-tuple-element.21.refs_0_, bf16[400,128]{1,0:T(8,128)(2,1)S(1)} %collective-permute-done.1.refs_1_, bf16[400,128]{1,0:T(8,128)(2,1)S(1)} %collective-permute-done.2.refs_2_, ...), custom_call_target="tpu_custom_call" | custom-call | tf_op jit(solution)/shard_map/back_project/pallas_call | solution.py:227
Async XLA Ops:
  0.6 1.9 %copy-start = (bf16[6,32,64,128]{3,2,1,0:T(8,128)(2,1)S(1)}, bf16[6,32,64,128]{3,2,1,0:T(8,128)(2,1)}, u32[]{:S(2)}) copy-start(bf16[6,32,64,128]{3,2,1,0:T(8,128)(2,1)} %param.6) | copy-start | bytes 9437188
  2.5 0.7 copy-start.2
  3.2 0.7 copy-start.3
  3.9 18.0 %copy-start.1 = (f32[2,128,256]{2,1,0:T(8,128)S(1)}, f32[2,128,256]{2,1,0:T(8,128)}, u32[]{:S(2)}) copy-start(f32[2,128,256]{2,1,0:T(8,128)} %measured_ref.3) | copy-start | bytes 786436
  3.9 26.6 %copy-start.5 = (s32[6,2]{0,1:T(2,128)S(1)}, s32[6,2]{0,1:T(2,128)}, u32[]{:S(2)}) copy-start(s32[6,2]{0,1:T(2,128)} %param.10) | copy-start | bytes 148
  11.4 36.2 %copy-start.6 = (f32[2]{0:T(128)S(1)}, f32[2]{0:T(128)}, u32[]{:S(2)}) copy-start(f32[2]{0:T(128)} %defocus_ref.1) | copy-start | bytes 28
  15.7 8.4 %collective-permute-start.3 = (bf16[400,128]{1,0:T(8,128)(2,1)S(1)}, bf16[400,128]{1,0:T(8,128)(2,1)S(1)}, u32[]{:S(2)}, u32[]{:S(2)}) collective-permute-start(bf16[400,128]{1,0:T(8,128)(2,1)S(1)} %get-tuple-element.24), channel_id=1, source_target_pairs={{0,24},{8,0},{16,8},{24,16},{1,25},{9,1},{17,9},{25,17},{2,26},{10... | collective-permute-start | bytes 307208 | tf_op jit(solution)/shard_map/ppermute | solution.py:20
  20.9 7.3 %collective-permute-start.1 = (bf16[400,128]{1,0:T(8,128)(2,1)S(1)}, bf16[400,128]{1,0:T(8,128)(2,1)S(1)}, u32[]{:S(2)}, u32[]{:S(2)}) collective-permute-start(bf16[400,128]{1,0:T(8,128)(2,1)S(1)} %get-tuple-element.22), channel_id=1, source_target_pairs={{0,8},{8,16},{16,24},{24,0},{1,9},{9,17},{17,25},{25,1},{2,10},{10... | collective-permute-start | bytes 307208 | tf_op jit(solution)/shard_map/ppermute | solution.py:20
  20.9 9.6 %collective-permute-start.2 = (bf16[400,128]{1,0:T(8,128)(2,1)S(1)}, bf16[400,128]{1,0:T(8,128)(2,1)S(1)}, u32[]{:S(2)}, u32[]{:S(2)}) collective-permute-start(bf16[400,128]{1,0:T(8,128)(2,1)S(1)} %get-tuple-element.23), channel_id=1, source_target_pairs={{0,16},{8,24},{16,0},{24,8},{1,17},{9,25},{17,1},{25,9},{2,18},{10... | collective-permute-start | bytes 307208 | tf_op jit(solution)/shard_map/ppermute | solution.py:20
  21.8 21.3 %collective-permute-start = (f32[2,128,256]{2,1,0:T(8,128)S(1)}, f32[2,128,256]{2,1,0:T(8,128)S(1)}, u32[]{:S(2)}, u32[]{:S(2)}) collective-permute-start(f32[2,128,256]{2,1,0:T(8,128)S(1)} %copy-done.1), channel_id=1, source_target_pairs={{0,7},{1,0},{2,1},{3,2},{4,3},{5,4},{6,5},{7,6},{8,15},{9,8},{10,9... | collective-permute-start | bytes 786440 | tf_op jit(solution)/shard_map/ppermute | solution.py:20
  31.8 5.2 %collective-permute-start.4 = (bf16[336,128]{1,0:T(8,128)(2,1)S(1)}, bf16[336,128]{1,0:T(8,128)(2,1)S(1)}, u32[]{:S(2)}, u32[]{:S(2)}) collective-permute-start(bf16[336,128]{1,0:T(8,128)(2,1)S(1)} %get-tuple-element.26), channel_id=1, source_target_pairs={{0,1},{1,2},{2,3},{3,4},{4,5},{5,6},{6,7},{7,0},{8,9},{9,10},{10,1... | collective-permute-start | bytes 258056 | tf_op jit(solution)/shard_map/ppermute | solution.py:20
  31.9 6.4 %collective-permute-start.5 = (bf16[336,128]{1,0:T(8,128)(2,1)S(1)}, bf16[336,128]{1,0:T(8,128)(2,1)S(1)}, u32[]{:S(2)}, u32[]{:S(2)}) collective-permute-start(bf16[336,128]{1,0:T(8,128)(2,1)S(1)} %get-tuple-element.27), channel_id=1, source_target_pairs={{0,2},{1,3},{2,4},{3,5},{4,6},{5,7},{6,0},{7,1},{8,10},{9,11},{10,... | collective-permute-start | bytes 258056 | tf_op jit(solution)/shard_map/ppermute | solution.py:20
  33.4 7.6 %collective-permute-start.6 = (bf16[336,128]{1,0:T(8,128)(2,1)S(1)}, bf16[336,128]{1,0:T(8,128)(2,1)S(1)}, u32[]{:S(2)}, u32[]{:S(2)}) collective-permute-start(bf16[336,128]{1,0:T(8,128)(2,1)S(1)} %get-tuple-element.28), channel_id=1, source_target_pairs={{0,3},{1,4},{2,5},{3,6},{4,7},{5,0},{6,1},{7,2},{8,11},{9,12},{10,... | collective-permute-start | bytes 258056 | tf_op jit(solution)/shard_map/ppermute | solution.py:20
  35.7 5.8 %collective-permute-start.7 = (bf16[336,128]{1,0:T(8,128)(2,1)S(1)}, bf16[336,128]{1,0:T(8,128)(2,1)S(1)}, u32[]{:S(2)}, u32[]{:S(2)}) collective-permute-start(bf16[336,128]{1,0:T(8,128)(2,1)S(1)} %get-tuple-element.29), channel_id=1, source_target_pairs={{0,4},{1,5},{2,6},{3,7},{4,0},{5,1},{6,2},{7,3},{8,12},{9,13},{10,... | collective-permute-start | bytes 258056 | tf_op jit(solution)/shard_map/ppermute | solution.py:20
  37.0 5.2 %collective-permute-start.8 = (bf16[336,128]{1,0:T(8,128)(2,1)S(1)}, bf16[336,128]{1,0:T(8,128)(2,1)S(1)}, u32[]{:S(2)}, u32[]{:S(2)}) collective-permute-start(bf16[336,128]{1,0:T(8,128)(2,1)S(1)} %get-tuple-element.30), channel_id=1, source_target_pairs={{0,5},{1,6},{2,7},{3,0},{4,1},{5,2},{6,3},{7,4},{8,13},{9,14},{10,... | collective-permute-start | bytes 258056 | tf_op jit(solution)/shard_map/ppermute | solution.py:20
  38.3 4.7 %collective-permute-start.9 = (bf16[336,128]{1,0:T(8,128)(2,1)S(1)}, bf16[336,128]{1,0:T(8,128)(2,1)S(1)}, u32[]{:S(2)}, u32[]{:S(2)}) collective-permute-start(bf16[336,128]{1,0:T(8,128)(2,1)S(1)} %get-tuple-element.31), channel_id=1, source_target_pairs={{0,6},{1,7},{2,0},{3,1},{4,2},{5,3},{6,4},{7,5},{8,14},{9,15},{10,... | collective-permute-start | bytes 258056 | tf_op jit(solution)/shard_map/ppermute | solution.py:20
  41.0 2.1 %collective-permute-start.10 = (bf16[336,128]{1,0:T(8,128)(2,1)S(1)}, bf16[336,128]{1,0:T(8,128)(2,1)S(1)}, u32[]{:S(2)}, u32[]{:S(2)}) collective-permute-start(bf16[336,128]{1,0:T(8,128)(2,1)S(1)} %get-tuple-element.32), channel_id=1, source_target_pairs={{0,7},{1,0},{2,1},{3,2},{4,3},{5,4},{6,5},{7,6},{8,15},{9,8},{10,9... | collective-permute-start | bytes 258056 | tf_op jit(solution)/shard_map/ppermute | solution.py:20
  44.9 5.8 %collective-permute-start.11 = (bf16[2,160,256]{2,1,0:T(8,128)(2,1)S(1)}, bf16[2,160,256]{2,1,0:T(8,128)(2,1)S(1)}, u32[]{:S(2)}, u32[]{:S(2)}) collective-permute-start(bf16[2,160,256]{2,1,0:T(8,128)(2,1)S(1)} %get-tuple-element.34), channel_id=1, source_target_pairs={{0,1},{1,2},{2,3},{3,4},{4,5},{5,6},{6,7},{7,0},{8,9},{9,10},{10,1... | collective-permute-start | bytes 491528 | tf_op jit(solution)/shard_map/ppermute | solution.py:20
  46.0 4.7 %collective-permute-start.12 = (bf16[2,160,256]{2,1,0:T(8,128)(2,1)S(1)}, bf16[2,160,256]{2,1,0:T(8,128)(2,1)S(1)}, u32[]{:S(2)}, u32[]{:S(2)}) collective-permute-start(bf16[2,160,256]{2,1,0:T(8,128)(2,1)S(1)} %get-tuple-element.35), channel_id=1, source_target_pairs={{0,7},{1,0},{2,1},{3,2},{4,3},{5,4},{6,5},{7,6},{8,15},{9,8},{10,9... | collective-permute-start | bytes 491528 | tf_op jit(solution)/shard_map/ppermute | solution.py:20
  48.9 27.3 %copy-start.4 = (f32[8]{0:T(128)S(1)}, f32[8]{0:T(128)}, u32[]{:S(2)}) copy-start(f32[8]{0:T(128)} %angle_ref.5) | copy-start | bytes 100
where the time goes:
time: 85.6 us; the launch traced here: 85.4 us
  Pallas kernels  31 us (36%)
  blocking collectives  19.9 us (23%)
  starting transfers between devices  15.8 us (18%)
  waiting for transfers between devices  14.7 us (17%)
  local copies, waits for them, and re-layouts  3.24 us (4%)
    all_to_all x1, blocking collectives, shards(): lax.all_to_all(cuts, ('tilt', 'tile'), split_axis=0, concat_axis=0, tiled...  19.9 us
    ppermute x13, starting transfers between devices, ring(): lax.ppermute(block, axis, [(i, (i + distance) % count) for i in range(cou...  15.8 us
    ppermute x13, waiting for transfers between devices, ring(): lax.ppermute(block, axis, [(i, (i + distance) % count) for i in range(cou...  14.7 us
    pallas_call x2, Pallas kernels, project(): pl.pallas_call(functools.partial(project_kernel, depth=depth, tilts=tilts...  11.8 us
    pallas_call x1, Pallas kernels, back_project(): pl.pallas_call(functools.partial(back_kernel, depth=depth, tilts=tilts, b...  9.14 us
    pallas_call x1, Pallas kernels, filter_and_cut(): pl.pallas_call(functools.partial(filter_kernel, height=height, capacity=c...  5.68 us
    unnamed x14, local copies, waits for them, and re-layouts  3.24 us
  transfers between devices with their start and end apart: 13, of which 11 were waited for; matrix products, arithmetic and copies ran while one was open for 0% of the time, Pallas kernels for 3%

commit v1 on v0

--- a/solution.py
+++ b/solution.py
@@ -20,6 +20,16 @@
     return lax.ppermute(block, axis, [(i, (i + distance) % count) for i in range(count)])
 
 
+def swap(block, axis, distance):
+    count = lax.axis_size(axis)
+    assert count & (count - 1) == 0
+    return lax.ppermute(block, axis, [(i, i ^ distance) for i in range(count)])
+
+
+def far(block):
+    return pltpu.with_memory_space_constraint(block, pltpu.HBM)
+
+
 def near(block):
     return pltpu.with_memory_space_constraint(block, pltpu.VMEM)
 
@@ -48,10 +58,10 @@
 def tap_block(apart, sine, layer, depth):
     shift = (layer.astype(F32) - (depth - 1) / 2.0) * sine
     lower = jnp.floor(shift)
-    copies = apart.shape[0] // sine.shape[0]
+    copies = apart.shape[0] // (2 * sine.shape[0])
 
     def filled(value):
-        return jnp.concatenate([value.astype(BF)] * copies, axis=0)
+        return jnp.concatenate([jnp.concatenate([value] * 2, axis=0).astype(BF)] * copies, axis=0)
 
     def weight(offset):
         return filled(jnp.maximum(0.0, 1.0 - jnp.abs(offset - shift)))
@@ -92,14 +102,21 @@
         lhs, wide = refs[len(ks)], refs[len(ks) + 1]
         rows, layers, width = vol_ref.shape
         wide[...] = vol_ref[...].reshape(rows * layers, width).astype(F32)
-        for z in range(layers):
-            lhs[:, z * width : (z + 1) * width] = wide[pl.ds(z, rows, stride=layers), :].astype(BF)
+
+        def pair_at(z):
+            pair = [wide[pl.ds(z + h, rows, stride=layers), :].astype(BF) for h in range(2)]
+            pair = jnp.concatenate(pair, axis=1)
+            lhs[:, z * width : (z + 2) * width] = pair
+            return pair
     else:
         lhs = vol_ref
         rows = lhs.shape[0]
         width = outs[0].shape[1]
         layers = lhs.shape[1] // width
 
+        def pair_at(z):
+            return lhs[:, z * width : (z + 2) * width]
+
     @pl.when(step == 0)
     def _():
         total[...] = jnp.zeros_like(total)
@@ -108,10 +125,14 @@
     apart = iota_apart((width, width), 1, 0)
 
     def block(k, z, t):
-        sine = sines[lax.rem(me + k, groups) * tilts + t]
+        sine = sines[(me ^ k) * tilts + t]
         return tap_block(apart, sine, step * layers + z, depth)
 
+    following = pair_at(0)
     for z in range(0, layers, 2):
+        pair = following
+        if z + 2 < layers:
+            following = pair_at(z + 2)
         for i, k in enumerate(ks):
             table = jnp.concatenate(
                 [
@@ -121,9 +142,7 @@
                 axis=0,
             )
             span = slice(i * tilts * width, (i + 1) * tilts * width)
-            total[:, span] += jnp.dot(
-                lhs[:, z * width : (z + 2) * width], table, preferred_element_type=F32
-            )
+            total[:, span] += jnp.dot(pair, table, preferred_element_type=F32)
 
     @pl.when(step == pl.num_programs(0) - 1)
     def _():
@@ -163,7 +182,7 @@
         scratch_shapes=([pltpu.VMEM((rows * layers, width), F32)] if first else [])
         + [
             pltpu.VMEM((rows, len(ks) * tilts * width), F32),
-            pltpu.VMEM((groups * tilts, 16, width), F32),
+            pltpu.VMEM((groups * tilts, 8, width), F32),
         ],
         compiler_params=GRANT,
         name="project_first" if first else "project_rest",
@@ -186,7 +205,7 @@
         ahead = lax.broadcasted_iota(jnp.int32, (slab_rows, length), 1)
         ahead = (ahead - lax.broadcasted_iota(jnp.int32, (slab_rows, length), 0)).astype(F32)
         for k in range(groups):
-            group = lax.rem(me + groups - k, groups)
+            group = (me ^ k)
             for t in range(tilts):
                 picks = []
                 for b in range(boxes):
@@ -198,7 +217,7 @@
                 ).astype(BF)
 
     def block(k, t, z):
-        sine = sines[lax.rem(me + groups - k, groups) * tilts + t]
+        sine = sines[(me ^ k) * tilts + t]
         return tap_block(apart, sine, step * layers + z, depth)
 
     flat = out_ref.reshape(rows * layers, width)
@@ -236,7 +255,7 @@
         out_specs=pl.BlockSpec((rows, layers, width), lambda i: (0, i, 0)),
         scratch_shapes=[
             pltpu.VMEM((rows, groups * tilts * width), BF),
-            pltpu.VMEM((groups * tilts, 16, width), F32),
+            pltpu.VMEM((groups * tilts, 8, width), F32),
         ],
         compiler_params=GRANT,
         name="back_project",
@@ -265,7 +284,7 @@
         item_ref[slot + margin] = n
         within_ref[slot + margin] = row_ref[t, b] - strip * strip_rows + t * strip_rows
         left_ref[slot + margin] = col_ref[t, b]
-    sources = [lax.rem(my_tilt + groups - k, groups) for k in range(groups)]
+    sources = [my_tilt ^ k for k in range(groups)]
 
     def slab_of(k, item, begin, size):
         start = pl.multiple_of(jnp.maximum(item, 0) * slab_rows + begin, 16)
@@ -274,7 +293,7 @@
 
     for d in range(tile_count):
         out = outs[d]
-        strip = lax.rem(my_tile + d, tile_count)
+        strip = my_tile ^ d
         metas = []
 
         def item_at(offset, r):
@@ -523,7 +542,7 @@
     column = iota_apart((image_width, width), 0, 1)
     meta = capacity * (height + 2 * REACH)
     for d, parcel in enumerate(parcels):
-        sender = lax.rem(my_tile + tile_count - d, tile_count)
+        sender = my_tile ^ d
         for r in range(capacity):
             top = parcel[meta + 2 * r : meta + 2 * r + 1, :].astype(F32)
             picks = []
@@ -571,22 +590,22 @@
     height, rows = slab_rows * groups, boxes * slab_rows
     capacity = max(2, -(-boxes * tilts // tile_count))
     assert tilts * strip_rows <= 256 and tile_count * capacity <= 256
-    rows_of, cols_of = row_offsets.T, col_offsets.T
+    rows_of, cols_of, angles = far(row_offsets.T), far(col_offsets.T), far(angles)
     after = ring(measured, "tile", -1)
     kernel = transfer_tables(defocus, image_width)
     slabs = [None] * groups
-    volume = volumes.reshape(rows, depth, width)
+    volume = far(volumes.reshape(rows, depth, width))
     half = groups // 2 + 1
     early, late = tuple(range(1, half)), (*range(half, groups), 0)
     sizes = (depth, width, strip_rows, capacity)
     *parts, flat = project(volume, rows_of, angles, tilts, groups, early, True, *sizes)
     for k, part in zip(early, parts, strict=True):
-        slabs[k] = ring(part, "tilt", k)
+        slabs[k] = swap(part, "tilt", k)
     parts = project(flat, rows_of, angles, tilts, groups, late, False, *sizes)
     for k, part in zip(late, parts, strict=True):
-        slabs[k] = ring(part, "tilt", k) if k else part
+        slabs[k] = swap(part, "tilt", k) if k else part
     parcels = pack(slabs, rows_of, cols_of, slab_rows, tile_count, strip_rows, capacity)
-    parcels = [p if d == 0 else ring(p, "tile", d) for d, p in enumerate(parcels)]
+    parcels = [p if d == 0 else swap(p, "tile", d) for d, p in enumerate(parcels)]
     canvas, onward, backward = place(measured, after, parcels, height, capacity)
     above, below = ring(onward, "tile", 1), ring(backward, "tile", -1)
     residual, cuts = filter_and_cut(

time: 85.6 us -> 80.7 us (0.943)
  local copies, waits for them, and re-layouts: 3.24 us -> 0.01 us
  Pallas kernels: 31 us -> 28.5 us
  starting transfers between devices: 15.8 us -> 17 us
    ppermute x0 -> x10, starting transfers between devices: none -> 13 us  [swap(): return lax.ppermute(block, axis, [(i, i ^ distance) for i in range(count)])]
    ppermute x13 -> x3, waiting for transfers between devices: 14.7 us -> 2.42 us  [ring(): lax.ppermute(block, axis, [(i, (i + distance) % count) for i in range(cou...]
    ppermute x0 -> x10, waiting for transfers between devices: none -> 12.3 us  [swap(): return lax.ppermute(block, axis, [(i, i ^ distance) for i in range(count)])]
    ppermute x13 -> x3, starting transfers between devices: 15.8 us -> 3.99 us  [ring(): lax.ppermute(block, axis, [(i, (i + distance) % count) for i in range(cou...]
    unnamed x14 -> x4, local copies, waits for them, and re-layouts: 3.24 us -> 0.01 us
    pallas_call x2, Pallas kernels: 11.8 us -> 9.72 us  [project(): pl.pallas_call(functools.partial(project_kernel, depth=depth, tilts=tilts...]
  transfers between devices with their start and end apart: 13 -> 13, of which waited for: 11 -> 8; matrix products, arithmetic and copies ran while one was open for 0% -> 0% of each run, Pallas kernels for 3% -> 4%
where the time goes in v1:
time: 80.7 us; the launch traced here: 80.5 us
  Pallas kernels  28.5 us (35%)
  blocking collectives  19.6 us (24%)
  starting transfers between devices  17 us (21%)
  waiting for transfers between devices  14.7 us (18%)
    all_to_all x1, blocking collectives, shards(): lax.all_to_all(cuts, ('tilt', 'tile'), split_axis=0, concat_axis=0, tiled...  19.6 us
    ppermute x10, starting transfers between devices, swap(): return lax.ppermute(block, axis, [(i, i ^ distance) for i in range(count)])  13 us
    ppermute x10, waiting for transfers between devices, swap(): return lax.ppermute(block, axis, [(i, i ^ distance) for i in range(count)])  12.3 us
    pallas_call x2, Pallas kernels, project(): pl.pallas_call(functools.partial(project_kernel, depth=depth, tilts=tilts...  9.72 us
    pallas_call x1, Pallas kernels, back_project(): pl.pallas_call(functools.partial(back_kernel, depth=depth, tilts=tilts, b...  8.51 us
    pallas_call x1, Pallas kernels, filter_and_cut(): pl.pallas_call(functools.partial(filter_kernel, height=height, capacity=c...  5.64 us
    ppermute x3, starting transfers between devices, ring(): lax.ppermute(block, axis, [(i, (i + distance) % count) for i in range(cou...  3.99 us
    ppermute x3, waiting for transfers between devices, ring(): lax.ppermute(block, axis, [(i, (i + distance) % count) for i in range(cou...  2.42 us
  transfers between devices with their start and end apart: 13, of which 8 were waited for; matrix products, arithmetic and copies ran while one was open for 0% of the time, Pallas kernels for 4%

profile of v1, /device:TPU:0, one launch (start us, length us, event | category | flops | bytes accessed | tf_op | source)
XLA Modules:
  0.0 80.5 jit_solution(12014432951797048331)
XLA Ops:
  0.6 0.0 copy-start
  0.6 5.9 %project_first.1 = (bf16[400,128]{1,0:T(8,128)(2,1)S(1)}, bf16[400,128]{1,0:T(8,128)(2,1)S(1)}, bf16[192,8192]{1,0:T(8,128)(2,1)S(1)}) custom-call(s32[2,6]{1,0:T(2,128)} %bitcast.10, f32[8]{0:T(128)} %angle_ref.5, bf16[192,64,128]{2,1,0:T(8,128)(2,1)} %bitcast.9), custom_call_target="tpu_custom_call" | custom-call | tf_op jit(solution)/shard_map/project_first/pallas_call | solution.py:165
  6.5 0.0 copy-start.1
  6.5 3.9 %project_rest.1 = (bf16[400,128]{1,0:T(8,128)(2,1)S(1)}, bf16[400,128]{1,0:T(8,128)(2,1)S(1)}) custom-call(s32[2,6]{1,0:T(2,128)} %bitcast.11, f32[8]{0:T(128)} %angle_ref.5, bf16[192,8192]{1,0:T(8,128)(2,1)S(1)} %get-tuple-element.20.vol_ref), custom_call_target="tpu_custom_call" | custom-call | tf_op jit(solution)/shard_map/project_rest/pallas_call | solution.py:165
  10.4 5.1 %collective-permute-start.3 = (bf16[400,128]{1,0:T(8,128)(2,1)S(1)}, bf16[400,128]{1,0:T(8,128)(2,1)S(1)}, u32[]{:S(2)}, u32[]{:S(2)}) collective-permute-start(bf16[400,128]{1,0:T(8,128)(2,1)S(1)} %get-tuple-element.24), channel_id=1, source_target_pairs={{0,24},{8,16},{16,8},{24,0},{1,25},{9,17},{17,9},{25,1},{2,26},{10... | collective-permute-start | bytes 307208 | tf_op jit(solution)/shard_map/ppermute | solution.py:26
  15.5 0.0 collective-permute-start.1
  15.5 0.6 collective-permute-start.2
  16.1 0.0 copy-done
  16.1 1.3 %collective-permute-start = (f32[2,128,256]{2,1,0:T(8,128)S(1)}, f32[2,128,256]{2,1,0:T(8,128)S(1)}, u32[]{:S(2)}, u32[]{:S(2)}) collective-permute-start(f32[2,128,256]{2,1,0:T(8,128)S(1)} %copy-done), channel_id=1, source_target_pairs={{0,7},{1,0},{2,1},{3,2},{4,3},{5,4},{6,5},{7,6},{8,15},{9,8},{10,9... | collective-permute-start | bytes 786440 | tf_op jit(solution)/shard_map/ppermute | solution.py:20
  17.5 1.8 %collective-permute-done.3.refs_3_ = bf16[400,128]{1,0:T(8,128)(2,1)S(1)} collective-permute-done((bf16[400,128]{1,0:T(8,128)(2,1)S(1)}, bf16[400,128]{1,0:T(8,128)(2,1)S(1)}, u32[]{:S(2)}, u32[]{:S(2)}) %collective-permute-start.3) | collective-permute-done | bytes 102432 | tf_op jit(solution)/shard_map/ppermute | solution.py:26
  19.3 2.4 %collective-permute-done.1.refs_1_ = bf16[400,128]{1,0:T(8,128)(2,1)S(1)} collective-permute-done((bf16[400,128]{1,0:T(8,128)(2,1)S(1)}, bf16[400,128]{1,0:T(8,128)(2,1)S(1)}, u32[]{:S(2)}, u32[]{:S(2)}) %collective-permute-start.1) | collective-permute-done | bytes 102432 | tf_op jit(solution)/shard_map/ppermute | solution.py:26
  21.7 2.4 %collective-permute-done.2.refs_2_ = bf16[400,128]{1,0:T(8,128)(2,1)S(1)} collective-permute-done((bf16[400,128]{1,0:T(8,128)(2,1)S(1)}, bf16[400,128]{1,0:T(8,128)(2,1)S(1)}, u32[]{:S(2)}, u32[]{:S(2)}) %collective-permute-start.2) | collective-permute-done | bytes 102432 | tf_op jit(solution)/shard_map/ppermute | solution.py:26
  24.1 1.6 %pack.1 = (bf16[336,128]{1,0:T(8,128)(2,1)S(1)}, bf16[336,128]{1,0:T(8,128)(2,1)S(1)}, bf16[336,128]{1,0:T(8,128)(2,1)S(1)}, bf16[336,128]{1,0:T(8,128)(2,1)S(1)...) custom-call(s32[2,6]{1,0:T(2,128)} %bitcast.12, ...), custom_call_target="tpu_custom_call" | custom-call | tf_op jit(solution)/shard_map/pack/pallas_call | solution.py:328
  25.7 0.1 collective-permute-start.4
  25.8 1.5 %collective-permute-start.5 = (bf16[336,128]{1,0:T(8,128)(2,1)S(1)}, bf16[336,128]{1,0:T(8,128)(2,1)S(1)}, u32[]{:S(2)}, u32[]{:S(2)}) collective-permute-start(bf16[336,128]{1,0:T(8,128)(2,1)S(1)} %get-tuple-element.27), channel_id=1, source_target_pairs={{0,2},{1,3},{2,0},{3,1},{4,6},{5,7},{6,4},{7,5},{8,10},{9,11},{10,... | collective-permute-start | bytes 258056 | tf_op jit(solution)/shard_map/ppermute | solution.py:26
  27.3 0.3 collective-permute-start.6
  27.6 1.5 %collective-permute-start.7 = (bf16[336,128]{1,0:T(8,128)(2,1)S(1)}, bf16[336,128]{1,0:T(8,128)(2,1)S(1)}, u32[]{:S(2)}, u32[]{:S(2)}) collective-permute-start(bf16[336,128]{1,0:T(8,128)(2,1)S(1)} %get-tuple-element.29), channel_id=1, source_target_pairs={{0,4},{1,5},{2,6},{3,7},{4,0},{5,1},{6,2},{7,3},{8,12},{9,13},{10,... | collective-permute-start | bytes 258056 | tf_op jit(solution)/shard_map/ppermute | solution.py:26
  29.1 0.0 collective-permute-done.4.refs_1_
  29.1 0.2 collective-permute-start.8
  29.3 1.8 %collective-permute-done.5.refs_2_ = bf16[336,128]{1,0:T(8,128)(2,1)S(1)} collective-permute-done((bf16[336,128]{1,0:T(8,128)(2,1)S(1)}, bf16[336,128]{1,0:T(8,128)(2,1)S(1)}, u32[]{:S(2)}, u32[]{:S(2)}) %collective-permute-start.5) | collective-permute-done | bytes 86048 | tf_op jit(solution)/shard_map/ppermute | solution.py:26
  31.1 2.6 %collective-permute-start.9 = (bf16[336,128]{1,0:T(8,128)(2,1)S(1)}, bf16[336,128]{1,0:T(8,128)(2,1)S(1)}, u32[]{:S(2)}, u32[]{:S(2)}) collective-permute-start(bf16[336,128]{1,0:T(8,128)(2,1)S(1)} %get-tuple-element.31), channel_id=1, source_target_pairs={{0,6},{1,7},{2,4},{3,5},{4,2},{5,3},{6,0},{7,1},{8,14},{9,15},{10,... | collective-permute-start | bytes 258056 | tf_op jit(solution)/shard_map/ppermute | solution.py:26
  33.7 0.0 collective-permute-done.6.refs_3_
  33.7 1.0 %collective-permute-start.10 = (bf16[336,128]{1,0:T(8,128)(2,1)S(1)}, bf16[336,128]{1,0:T(8,128)(2,1)S(1)}, u32[]{:S(2)}, u32[]{:S(2)}) collective-permute-start(bf16[336,128]{1,0:T(8,128)(2,1)S(1)} %get-tuple-element.32), channel_id=1, source_target_pairs={{0,7},{1,6},{2,5},{3,4},{4,3},{5,2},{6,1},{7,0},{8,15},{9,14},{10,... | collective-permute-start | bytes 258056 | tf_op jit(solution)/shard_map/ppermute | solution.py:26
  34.7 0.0 collective-permute-done.7.refs_4_
  34.7 0.2 collective-permute-done.8.refs_5_
  34.9 1.6 %collective-permute-done.9.refs_6_ = bf16[336,128]{1,0:T(8,128)(2,1)S(1)} collective-permute-done((bf16[336,128]{1,0:T(8,128)(2,1)S(1)}, bf16[336,128]{1,0:T(8,128)(2,1)S(1)}, u32[]{:S(2)}, u32[]{:S(2)}) %collective-permute-start.9) | collective-permute-done | bytes 86048 | tf_op jit(solution)/shard_map/ppermute | solution.py:26
  36.5 2.1 %collective-permute-done.10.refs_7_ = bf16[336,128]{1,0:T(8,128)(2,1)S(1)} collective-permute-done((bf16[336,128]{1,0:T(8,128)(2,1)S(1)}, bf16[336,128]{1,0:T(8,128)(2,1)S(1)}, u32[]{:S(2)}, u32[]{:S(2)}) %collective-permute-start.10) | collective-permute-done | bytes 86048 | tf_op jit(solution)/shard_map/ppermute | solution.py:26
  38.6 0.0 collective-permute-done.after_ref
  38.6 1.7 %place.1 = (f32[2,288,256]{2,1,0:T(8,128)S(1)}, bf16[2,160,256]{2,1,0:T(8,128)(2,1)S(1)}, bf16[2,160,256]{2,1,0:T(8,128)(2,1)S(1)}) custom-call(f32[2,128,256]{2,1,0:T(8,128)S(1)} %copy-done, f32[2,128,256]{2,1,0:T(8,128)S(1)} %collective-permute-done.after_ref, bf16[336,128]{1,0:T(8,128)(2,1)S(1)} %get-tuple-element.25.refs_0_, ...), custom_call_target="tpu_custom_call" | custom-call | tf_op jit(solution)/shard_map/place/pallas_call | solution.py:420
  40.3 0.0 collective-permute-start.11
  40.3 2.6 %collective-permute-start.12 = (bf16[2,160,256]{2,1,0:T(8,128)(2,1)S(1)}, bf16[2,160,256]{2,1,0:T(8,128)(2,1)S(1)}, u32[]{:S(2)}, u32[]{:S(2)}) collective-permute-start(bf16[2,160,256]{2,1,0:T(8,128)(2,1)S(1)} %get-tuple-element.35), channel_id=1, source_target_pairs={{0,7},{1,0},{2,1},{3,2},{4,3},{5,4},{6,5},{7,6},{8,15},{9,8},{10,9... | collective-permute-start | bytes 491528 | tf_op jit(solution)/shard_map/ppermute | solution.py:20
  42.9 0.0 copy-done.1
  42.9 1.3 %transfer.1.table_ref = bf16[2,9,256,256]{3,2,1,0:T(8,128)(2,1)S(1)} custom-call(f32[2]{0:T(128)S(1)} %copy-done.1), custom_call_target="tpu_custom_call" | custom-call | tf_op jit(solution)/shard_map/transfer/pallas_call | solution.py:475
  44.3 2.4 %collective-permute-done.11.above_ref = bf16[2,160,256]{2,1,0:T(8,128)(2,1)S(1)} collective-permute-done((bf16[2,160,256]{2,1,0:T(8,128)(2,1)S(1)}, bf16[2,160,256]{2,1,0:T(8,128)(2,1)S(1)}, u32[]{:S(2)}, u32[]{:S(2)}) %collective-permute-start.11) | collective-permute-done | bytes 163872 | tf_op jit(solution)/shard_map/ppermute | solution.py:20
  46.7 0.0 collective-permute-done.12.below_ref
  46.7 5.6 %filter_and_cut.1 = (f32[2,128,256]{2,1,0:T(8,128)}, bf16[4,8,64,128]{3,2,1,0:T(8,128)(2,1)S(1)}) custom-call(f32[2,288,256]{2,1,0:T(8,128)S(1)} %get-tuple-element.33.canvas_ref, bf16[2,160,256]{2,1,0:T(8,128)(2,1)S(1)} %collective-permute-done.11.above_ref, bf16[2,160,256]{2,1,0:T(8,128)(2,1)S(1)} %collective-permute-done.12.below_ref, ...), custom_call_target="tpu_custom_call" | custom-call | tf_op jit(solution)/shard_map/filter_and_cut/pallas_call | solution.py:572
  52.3 19.6 %all_to_all.5 = bf16[32,64,128]{2,1,0:T(8,128)(2,1)S(1)} all-to-all(bf16[32,64,128]{2,1,0:T(8,128)(2,1)S(1)} %bitcast.7), channel_id=1, replica_groups=mesh['tilt'=4,'tile'=8] {'tilt','tile'}, dimensions={0} | all-to-all | bytes 1048576 | tf_op jit(solution)/shard_map/all_to_all | solution.py:615
  72.0 8.5 %back_project.1 = f32[192,64,128]{2,1,0:T(8,128)} custom-call(f32[8]{0:T(128)} %angle_ref.5, bf16[4,512,128]{2,1,0:T(8,128)(2,1)S(1)} %bitcast.6, bf16[400,128]{1,0:T(8,128)(2,1)S(1)} %get-tuple-element.21.refs_0_, bf16[400,128]{1,0:T(8,128)(2,1)S(1)} %collective-permute-done.1.refs_1_, bf16[400,128]{1,0:T(8,128)(2,1)S(1)} %collective-permute-done.2.refs_2_, ...), custom_call_target="tpu_custom_call" | custom-call | tf_op jit(solution)/shard_map/back_project/pallas_call | solution.py:246
Async XLA Ops:
  0.6 15.5 %copy-start = (f32[2,128,256]{2,1,0:T(8,128)S(1)}, f32[2,128,256]{2,1,0:T(8,128)}, u32[]{:S(2)}) copy-start(f32[2,128,256]{2,1,0:T(8,128)} %measured_ref.3) | copy-start | bytes 786436
  6.5 36.4 %copy-start.1 = (f32[2]{0:T(128)S(1)}, f32[2]{0:T(128)}, u32[]{:S(2)}) copy-start(f32[2]{0:T(128)} %defocus_ref.1) | copy-start | bytes 28
  10.4 8.9 %collective-permute-start.3 = (bf16[400,128]{1,0:T(8,128)(2,1)S(1)}, bf16[400,128]{1,0:T(8,128)(2,1)S(1)}, u32[]{:S(2)}, u32[]{:S(2)}) collective-permute-start(bf16[400,128]{1,0:T(8,128)(2,1)S(1)} %get-tuple-element.24), channel_id=1, source_target_pairs={{0,24},{8,16},{16,8},{24,0},{1,25},{9,17},{17,9},{25,1},{2,26},{10... | collective-permute-start | bytes 307208 | tf_op jit(solution)/shard_map/ppermute | solution.py:26
  15.5 6.2 %collective-permute-start.1 = (bf16[400,128]{1,0:T(8,128)(2,1)S(1)}, bf16[400,128]{1,0:T(8,128)(2,1)S(1)}, u32[]{:S(2)}, u32[]{:S(2)}) collective-permute-start(bf16[400,128]{1,0:T(8,128)(2,1)S(1)} %get-tuple-element.22), channel_id=1, source_target_pairs={{0,8},{8,0},{16,24},{24,16},{1,9},{9,1},{17,25},{25,17},{2,10},{10... | collective-permute-start | bytes 307208 | tf_op jit(solution)/shard_map/ppermute | solution.py:26
  15.5 8.6 %collective-permute-start.2 = (bf16[400,128]{1,0:T(8,128)(2,1)S(1)}, bf16[400,128]{1,0:T(8,128)(2,1)S(1)}, u32[]{:S(2)}, u32[]{:S(2)}) collective-permute-start(bf16[400,128]{1,0:T(8,128)(2,1)S(1)} %get-tuple-element.23), channel_id=1, source_target_pairs={{0,16},{8,24},{16,0},{24,8},{1,17},{9,25},{17,1},{25,9},{2,18},{10... | collective-permute-start | bytes 307208 | tf_op jit(solution)/shard_map/ppermute | solution.py:26
  16.1 22.4 %collective-permute-start = (f32[2,128,256]{2,1,0:T(8,128)S(1)}, f32[2,128,256]{2,1,0:T(8,128)S(1)}, u32[]{:S(2)}, u32[]{:S(2)}) collective-permute-start(f32[2,128,256]{2,1,0:T(8,128)S(1)} %copy-done), channel_id=1, source_target_pairs={{0,7},{1,0},{2,1},{3,2},{4,3},{5,4},{6,5},{7,6},{8,15},{9,8},{10,9... | collective-permute-start | bytes 786440 | tf_op jit(solution)/shard_map/ppermute | solution.py:20
  25.7 3.5 %collective-permute-start.4 = (bf16[336,128]{1,0:T(8,128)(2,1)S(1)}, bf16[336,128]{1,0:T(8,128)(2,1)S(1)}, u32[]{:S(2)}, u32[]{:S(2)}) collective-permute-start(bf16[336,128]{1,0:T(8,128)(2,1)S(1)} %get-tuple-element.26), channel_id=1, source_target_pairs={{0,1},{1,0},{2,3},{3,2},{4,5},{5,4},{6,7},{7,6},{8,9},{9,8},{10,11... | collective-permute-start | bytes 258056 | tf_op jit(solution)/shard_map/ppermute | solution.py:26
  25.8 5.3 %collective-permute-start.5 = (bf16[336,128]{1,0:T(8,128)(2,1)S(1)}, bf16[336,128]{1,0:T(8,128)(2,1)S(1)}, u32[]{:S(2)}, u32[]{:S(2)}) collective-permute-start(bf16[336,128]{1,0:T(8,128)(2,1)S(1)} %get-tuple-element.27), channel_id=1, source_target_pairs={{0,2},{1,3},{2,0},{3,1},{4,6},{5,7},{6,4},{7,5},{8,10},{9,11},{10,... | collective-permute-start | bytes 258056 | tf_op jit(solution)/shard_map/ppermute | solution.py:26
  27.3 6.4 %collective-permute-start.6 = (bf16[336,128]{1,0:T(8,128)(2,1)S(1)}, bf16[336,128]{1,0:T(8,128)(2,1)S(1)}, u32[]{:S(2)}, u32[]{:S(2)}) collective-permute-start(bf16[336,128]{1,0:T(8,128)(2,1)S(1)} %get-tuple-element.28), channel_id=1, source_target_pairs={{0,3},{1,2},{2,1},{3,0},{4,7},{5,6},{6,5},{7,4},{8,11},{9,10},{10,... | collective-permute-start | bytes 258056 | tf_op jit(solution)/shard_map/ppermute | solution.py:26
  27.6 7.1 %collective-permute-start.7 = (bf16[336,128]{1,0:T(8,128)(2,1)S(1)}, bf16[336,128]{1,0:T(8,128)(2,1)S(1)}, u32[]{:S(2)}, u32[]{:S(2)}) collective-permute-start(bf16[336,128]{1,0:T(8,128)(2,1)S(1)} %get-tuple-element.29), channel_id=1, source_target_pairs={{0,4},{1,5},{2,6},{3,7},{4,0},{5,1},{6,2},{7,3},{8,12},{9,13},{10,... | collective-permute-start | bytes 258056 | tf_op jit(solution)/shard_map/ppermute | solution.py:26
  29.1 5.8 %collective-permute-start.8 = (bf16[336,128]{1,0:T(8,128)(2,1)S(1)}, bf16[336,128]{1,0:T(8,128)(2,1)S(1)}, u32[]{:S(2)}, u32[]{:S(2)}) collective-permute-start(bf16[336,128]{1,0:T(8,128)(2,1)S(1)} %get-tuple-element.30), channel_id=1, source_target_pairs={{0,5},{1,4},{2,7},{3,6},{4,1},{5,0},{6,3},{7,2},{8,13},{9,12},{10,... | collective-permute-start | bytes 258056 | tf_op jit(solution)/shard_map/ppermute | solution.py:26
  31.1 5.4 %collective-permute-start.9 = (bf16[336,128]{1,0:T(8,128)(2,1)S(1)}, bf16[336,128]{1,0:T(8,128)(2,1)S(1)}, u32[]{:S(2)}, u32[]{:S(2)}) collective-permute-start(bf16[336,128]{1,0:T(8,128)(2,1)S(1)} %get-tuple-element.31), channel_id=1, source_target_pairs={{0,6},{1,7},{2,4},{3,5},{4,2},{5,3},{6,0},{7,1},{8,14},{9,15},{10,... | collective-permute-start | bytes 258056 | tf_op jit(solution)/shard_map/ppermute | solution.py:26
  33.7 4.9 %collective-permute-start.10 = (bf16[336,128]{1,0:T(8,128)(2,1)S(1)}, bf16[336,128]{1,0:T(8,128)(2,1)S(1)}, u32[]{:S(2)}, u32[]{:S(2)}) collective-permute-start(bf16[336,128]{1,0:T(8,128)(2,1)S(1)} %get-tuple-element.32), channel_id=1, source_target_pairs={{0,7},{1,6},{2,5},{3,4},{4,3},{5,2},{6,1},{7,0},{8,15},{9,14},{10,... | collective-permute-start | bytes 258056 | tf_op jit(solution)/shard_map/ppermute | solution.py:26
  40.3 6.4 %collective-permute-start.11 = (bf16[2,160,256]{2,1,0:T(8,128)(2,1)S(1)}, bf16[2,160,256]{2,1,0:T(8,128)(2,1)S(1)}, u32[]{:S(2)}, u32[]{:S(2)}) collective-permute-start(bf16[2,160,256]{2,1,0:T(8,128)(2,1)S(1)} %get-tuple-element.34), channel_id=1, source_target_pairs={{0,1},{1,2},{2,3},{3,4},{4,5},{5,6},{6,7},{7,0},{8,9},{9,10},{10,1... | collective-permute-start | bytes 491528 | tf_op jit(solution)/shard_map/ppermute | solution.py:20
  40.3 6.4 %collective-permute-start.12 = (bf16[2,160,256]{2,1,0:T(8,128)(2,1)S(1)}, bf16[2,160,256]{2,1,0:T(8,128)(2,1)S(1)}, u32[]{:S(2)}, u32[]{:S(2)}) collective-permute-start(bf16[2,160,256]{2,1,0:T(8,128)(2,1)S(1)} %get-tuple-element.35), channel_id=1, source_target_pairs={{0,7},{1,0},{2,1},{3,2},{4,3},{5,4},{6,5},{7,6},{8,15},{9,8},{10,9... | collective-permute-start | bytes 491528 | tf_op jit(solution)/shard_map/ppermute | solution.py:20

commit v2 on v1

--- a/solution.py
+++ b/solution.py
@@ -293,7 +293,7 @@
 
     for d in range(tile_count):
         out = outs[d]
-        strip = my_tile ^ d
+        strip = lax.rem(my_tile + d, tile_count)
         metas = []
 
         def item_at(offset, r):
@@ -482,23 +482,48 @@
     )(defocus)
 
 
-def convolve(source, parts, table_ref, t, height):
-    rows = source.shape[0]
-    for i in range(HR + 1):
-        parts[i, :rows, :] = jnp.dot(source, table_ref[t, i], preferred_element_type=F32)
-    total = parts[0, HR : HR + height, :]
-    for i in range(1, HR + 1):
-        total = total + (
-            parts[i, HR + i : HR + i + height, :] + parts[i, HR - i : HR - i + height, :]
-        )
-    return total
+def products(source, parts, table_ref, t):
+    def one(i):
+        def emit():
+            parts[i, : source.shape[0], :] = jnp.dot(
+                source[...], table_ref[t, i], preferred_element_type=F32
+            )
+
+        return emit
+
+    return [one(i) for i in range(HR + 1)]
+
+
+def shifted_sums(parts, height, finish):
+    def one(begin):
+        def emit():
+            total = parts[0, HR + begin : HR + begin + 16, :]
+            for i in range(1, HR + 1):
+                for at in (HR + i + begin, HR - i + begin):
+                    total = total + parts[i, at : at + 16, :]
+            finish(begin, total)
+
+        return emit
+
+    return [one(begin) for begin in range(0, height, 16)]
+
+
+def emit_beside(first, second):
+    done = 0
+    for n, emit in enumerate(first):
+        emit()
+        upto = len(second) * (n + 1) // len(first)
+        for other in second[done:upto]:
+            other()
+        done = upto
 
 
 def filter_kernel(
     canvas_ref, above_ref, below_ref, measured_ref, after_ref, table_ref, *refs, height, capacity
 ):
-    tile_count = len(refs) - 4
-    parcels, (residual_ref, out_ref, parts, back) = refs[:tile_count], refs[tile_count:]
+    tile_count = len(refs) - 7
+    parcels = refs[:tile_count]
+    residual_ref, out_ref, parts, fields, known, rests, back = refs[tile_count:]
     groups = out_ref.shape[0]
     slab_rows = height // groups
     tilts, strip_rows, image_width = measured_ref.shape
@@ -514,35 +539,71 @@
 
     at_top, at_end = my_tile == 0, my_tile == tile_count - 1
     for t in range(tilts):
-        upper = jnp.where(at_top, 0.0, above_ref[t, :reach, :].astype(F32))
-        lower = jnp.where(at_end, 0.0, below_ref[t, :reach, :].astype(F32))
-        field = canvas_ref[t] + jnp.concatenate([upper, lower], axis=0)
-        field = jnp.where(inside(rows, -REACH), field, 0.0)
-        known = jnp.concatenate(
-            [
-                above_ref[t, reach : reach + HR, :].astype(F32)
-                + above_ref[t, reach + HR :, :].astype(F32),
-                measured_ref[t],
-                after_ref[t],
-                below_ref[t, reach : reach + HR, :].astype(F32)
-                + below_ref[t, reach + HR :, :].astype(F32),
-            ],
-            axis=0,
+        for half, (edge, none) in enumerate(((above_ref, at_top), (below_ref, at_end))):
+            for begin in range(0, reach, 16):
+                row = half * reach + begin
+                field = jnp.where(none, 0.0, edge[t, begin : begin + 16, :].astype(F32))
+                field = jnp.where(
+                    inside(16, row - REACH), field + canvas_ref[t, row : row + 16, :], 0.0
+                )
+                fields[t, row : row + 16, :] = field.astype(BF)
+        known[t, :HR, :] = above_ref[t, reach : reach + HR, :].astype(F32) + above_ref[
+            t, reach + HR :, :
+        ].astype(F32)
+        known[t, HR : HR + strip_rows, :] = measured_ref[t]
+        known[t, HR + strip_rows : HR + 2 * strip_rows, :] = after_ref[t]
+        known[t, HR + 2 * strip_rows :, :] = below_ref[t, reach : reach + HR, :].astype(
+            F32
+        ) + below_ref[t, reach + HR :, :].astype(F32)
+    count = rows - 2 * HR
+
+    def keep_residual(t):
+        def finish(begin, total):
+            rest = known[t, begin : begin + 16, :] - total
+            low, high = max(begin, HR), min(begin + 16, HR + strip_rows)
+            if low < high:
+                residual_ref[t, low - HR : high - HR, :] = rest[low - begin : high - begin]
+            rests[t, begin : begin + 16, :] = jnp.where(
+                inside(16, begin - HR), rest, 0.0
+            ).astype(BF)
+
+        return finish
+
+    def keep_back(t):
+        def finish(begin, total):
+            row = t * 2 * strip_rows + begin
+            back[row : row + 16, :] = jnp.where(inside(16, begin), total, 0.0).astype(BF)
+
+        return finish
+
+    stages = [
+        (
+            products(fields.at[t], parts.at[t], table_ref, t),
+            shifted_sums(parts.at[t], count, keep_residual(t)),
         )
-        count = rows - 2 * HR
-        rest = known - convolve(field.astype(BF), parts, table_ref, t, count)
-        residual_ref[t] = rest[HR : HR + strip_rows]
-        rest = jnp.where(inside(count, -HR), rest, 0.0)
-        count -= 2 * HR
-        image = convolve(rest.astype(BF), parts, table_ref, t, count)
-        back[t * count : (t + 1) * count, :] = jnp.where(inside(count, 0), image, 0.0).astype(BF)
+        for t in range(tilts)
+    ]
+    stages += [
+        (
+            products(rests.at[t], parts.at[t], table_ref, t),
+            shifted_sums(parts.at[t], count - 2 * HR, keep_back(t)),
+        )
+        for t in range(tilts)
+    ]
+    assert tilts > 1
+    waiting = []
+    for multiply, add in stages:
+        emit_beside(multiply, waiting)
+        waiting = add
+    for emit in waiting:
+        emit()
     width = parcels[0].shape[1]
     count = 2 * strip_rows
     apart = iota_apart((height, count), 1, 0)
     column = iota_apart((image_width, width), 0, 1)
     meta = capacity * (height + 2 * REACH)
     for d, parcel in enumerate(parcels):
-        sender = my_tile ^ d
+        sender = lax.rem(my_tile + tile_count - d, tile_count)
         for r in range(capacity):
             top = parcel[meta + 2 * r : meta + 2 * r + 1, :].astype(F32)
             picks = []
@@ -575,7 +636,10 @@
         in_specs=[whole] * (6 + tile_count),
         out_specs=[whole] * 2,
         scratch_shapes=[
-            pltpu.VMEM((HR + 1, rows, image_width), F32),
+            pltpu.VMEM((tilts, HR + 1, rows, image_width), F32),
+            pltpu.VMEM((tilts, rows, image_width), BF),
+            pltpu.VMEM((tilts, rows - 2 * HR, image_width), F32),
+            pltpu.VMEM((tilts, rows - 2 * HR, image_width), BF),
             pltpu.VMEM((tilts * 2 * strip_rows, image_width), BF),
         ],
         compiler_params=GRANT,
@@ -605,7 +669,7 @@
     for k, part in zip(late, parts, strict=True):
         slabs[k] = swap(part, "tilt", k) if k else part
     parcels = pack(slabs, rows_of, cols_of, slab_rows, tile_count, strip_rows, capacity)
-    parcels = [p if d == 0 else swap(p, "tile", d) for d, p in enumerate(parcels)]
+    parcels = [p if d == 0 else ring(p, "tile", d) for d, p in enumerate(parcels)]
     canvas, onward, backward = place(measured, after, parcels, height, capacity)
     above, below = ring(onward, "tile", 1), ring(backward, "tile", -1)
     residual, cuts = filter_and_cut(

time: 80.7 us -> 79.9 us (0.990)
  starting transfers between devices: 17 us -> 15.8 us
  waiting for transfers between devices: 14.7 us -> 13.7 us
  blocking collectives: 19.6 us -> 20.5 us
    ppermute x10 -> x3, starting transfers between devices: 13 us -> 5.75 us  [swap(): return lax.ppermute(block, axis, [(i, i ^ distance) for i in range(count)])]
    ppermute x3 -> x10, starting transfers between devices: 3.99 us -> 10 us  [ring(): lax.ppermute(block, axis, [(i, (i + distance) % count) for i in range(cou...]
    ppermute x10 -> x3, waiting for transfers between devices: 12.3 us -> 6.63 us  [swap(): return lax.ppermute(block, axis, [(i, i ^ distance) for i in range(count)])]
    ppermute x3 -> x10, waiting for transfers between devices: 2.42 us -> 7.12 us  [ring(): lax.ppermute(block, axis, [(i, (i + distance) % count) for i in range(cou...]
    all_to_all x1, blocking collectives: 19.6 us -> 20.5 us  [shards(): lax.all_to_all(cuts, ('tilt', 'tile'), split_axis=0, concat_axis=0, tiled...]
  transfers between devices with their start and end apart: 13 -> 13, of which waited for: 8 -> 11; matrix products, arithmetic and copies ran while one was open for 0% -> 0% of each run, Pallas kernels for 4% -> 4%
where the time goes in v2:
time: 79.9 us; the launch traced here: 79.6 us
  Pallas kernels  29 us (36%)
  blocking collectives  20.5 us (26%)
  starting transfers between devices  15.8 us (20%)
  waiting for transfers between devices  13.7 us (17%)
    all_to_all x1, blocking collectives, shards(): lax.all_to_all(cuts, ('tilt', 'tile'), split_axis=0, concat_axis=0, tiled...  20.5 us
    ppermute x10, starting transfers between devices, ring(): lax.ppermute(block, axis, [(i, (i + distance) % count) for i in range(cou...  10 us
    pallas_call x2, Pallas kernels, project(): pl.pallas_call(functools.partial(project_kernel, depth=depth, tilts=tilts...  9.72 us
    pallas_call x1, Pallas kernels, back_project(): pl.pallas_call(functools.partial(back_kernel, depth=depth, tilts=tilts, b...  8.5 us
    ppermute x10, waiting for transfers between devices, ring(): lax.ppermute(block, axis, [(i, (i + distance) % count) for i in range(cou...  7.12 us
    ppermute x3, waiting for transfers between devices, swap(): return lax.ppermute(block, axis, [(i, i ^ distance) for i in range(count)])  6.63 us
    pallas_call x1, Pallas kernels, filter_and_cut(): pl.pallas_call(functools.partial(filter_kernel, height=height, capacity=c...  6.13 us
    ppermute x3, starting transfers between devices, swap(): return lax.ppermute(block, axis, [(i, i ^ distance) for i in range(count)])  5.75 us
  transfers between devices with their start and end apart: 13, of which 11 were waited for; matrix products, arithmetic and copies ran while one was open for 0% of the time, Pallas kernels for 4%

profile of v2, /device:TPU:0, one launch (start us, length us, event | category | flops | bytes accessed | tf_op | source)
XLA Modules:
  0.0 79.6 jit_solution(440952291592708591)
XLA Ops:
  0.6 0.0 copy-start
  0.6 5.9 %project_first.1 = (bf16[400,128]{1,0:T(8,128)(2,1)S(1)}, bf16[400,128]{1,0:T(8,128)(2,1)S(1)}, bf16[192,8192]{1,0:T(8,128)(2,1)S(1)}) custom-call(s32[2,6]{1,0:T(2,128)} %bitcast.10, f32[8]{0:T(128)} %angle_ref.5, bf16[192,64,128]{2,1,0:T(8,128)(2,1)} %bitcast.9), custom_call_target="tpu_custom_call" | custom-call | tf_op jit(solution)/shard_map/project_first/pallas_call | solution.py:165
  6.5 0.0 copy-start.1
  6.5 3.9 %project_rest.1 = (bf16[400,128]{1,0:T(8,128)(2,1)S(1)}, bf16[400,128]{1,0:T(8,128)(2,1)S(1)}) custom-call(s32[2,6]{1,0:T(2,128)} %bitcast.11, f32[8]{0:T(128)} %angle_ref.5, bf16[192,8192]{1,0:T(8,128)(2,1)S(1)} %get-tuple-element.20.vol_ref), custom_call_target="tpu_custom_call" | custom-call | tf_op jit(solution)/shard_map/project_rest/pallas_call | solution.py:165
  10.4 5.1 %collective-permute-start.3 = (bf16[400,128]{1,0:T(8,128)(2,1)S(1)}, bf16[400,128]{1,0:T(8,128)(2,1)S(1)}, u32[]{:S(2)}, u32[]{:S(2)}) collective-permute-start(bf16[400,128]{1,0:T(8,128)(2,1)S(1)} %get-tuple-element.24), channel_id=1, source_target_pairs={{0,24},{8,16},{16,8},{24,0},{1,25},{9,17},{17,9},{25,1},{2,26},{10... | collective-permute-start | bytes 307208 | tf_op jit(solution)/shard_map/ppermute | solution.py:26
  15.5 0.0 collective-permute-start.1
  15.5 0.6 collective-permute-start.2
  16.1 0.0 copy-done
  16.1 1.3 %collective-permute-start = (f32[2,128,256]{2,1,0:T(8,128)S(1)}, f32[2,128,256]{2,1,0:T(8,128)S(1)}, u32[]{:S(2)}, u32[]{:S(2)}) collective-permute-start(f32[2,128,256]{2,1,0:T(8,128)S(1)} %copy-done), channel_id=1, source_target_pairs={{0,7},{1,0},{2,1},{3,2},{4,3},{5,4},{6,5},{7,6},{8,15},{9,8},{10,9... | collective-permute-start | bytes 786440 | tf_op jit(solution)/shard_map/ppermute | solution.py:20
  17.5 1.8 %collective-permute-done.3.refs_3_ = bf16[400,128]{1,0:T(8,128)(2,1)S(1)} collective-permute-done((bf16[400,128]{1,0:T(8,128)(2,1)S(1)}, bf16[400,128]{1,0:T(8,128)(2,1)S(1)}, u32[]{:S(2)}, u32[]{:S(2)}) %collective-permute-start.3) | collective-permute-done | bytes 102432 | tf_op jit(solution)/shard_map/ppermute | solution.py:26
  19.3 2.4 %collective-permute-done.1.refs_1_ = bf16[400,128]{1,0:T(8,128)(2,1)S(1)} collective-permute-done((bf16[400,128]{1,0:T(8,128)(2,1)S(1)}, bf16[400,128]{1,0:T(8,128)(2,1)S(1)}, u32[]{:S(2)}, u32[]{:S(2)}) %collective-permute-start.1) | collective-permute-done | bytes 102432 | tf_op jit(solution)/shard_map/ppermute | solution.py:26
  21.7 2.4 %collective-permute-done.2.refs_2_ = bf16[400,128]{1,0:T(8,128)(2,1)S(1)} collective-permute-done((bf16[400,128]{1,0:T(8,128)(2,1)S(1)}, bf16[400,128]{1,0:T(8,128)(2,1)S(1)}, u32[]{:S(2)}, u32[]{:S(2)}) %collective-permute-start.2) | collective-permute-done | bytes 102432 | tf_op jit(solution)/shard_map/ppermute | solution.py:26
  24.1 1.6 %pack.1 = (bf16[336,128]{1,0:T(8,128)(2,1)S(1)}, bf16[336,128]{1,0:T(8,128)(2,1)S(1)}, bf16[336,128]{1,0:T(8,128)(2,1)S(1)}, bf16[336,128]{1,0:T(8,128)(2,1)S(1)...) custom-call(s32[2,6]{1,0:T(2,128)} %bitcast.12, ...), custom_call_target="tpu_custom_call" | custom-call | tf_op jit(solution)/shard_map/pack/pallas_call | solution.py:328
  25.7 0.1 collective-permute-start.4
  25.8 1.5 %collective-permute-start.5 = (bf16[336,128]{1,0:T(8,128)(2,1)S(1)}, bf16[336,128]{1,0:T(8,128)(2,1)S(1)}, u32[]{:S(2)}, u32[]{:S(2)}) collective-permute-start(bf16[336,128]{1,0:T(8,128)(2,1)S(1)} %get-tuple-element.27), channel_id=1, source_target_pairs={{0,2},{1,3},{2,4},{3,5},{4,6},{5,7},{6,0},{7,1},{8,10},{9,11},{10,... | collective-permute-start | bytes 258056 | tf_op jit(solution)/shard_map/ppermute | solution.py:20
  27.3 2.4 %collective-permute-start.6 = (bf16[336,128]{1,0:T(8,128)(2,1)S(1)}, bf16[336,128]{1,0:T(8,128)(2,1)S(1)}, u32[]{:S(2)}, u32[]{:S(2)}) collective-permute-start(bf16[336,128]{1,0:T(8,128)(2,1)S(1)} %get-tuple-element.28), channel_id=1, source_target_pairs={{0,3},{1,4},{2,5},{3,6},{4,7},{5,0},{6,1},{7,2},{8,11},{9,12},{10,... | collective-permute-start | bytes 258056 | tf_op jit(solution)/shard_map/ppermute | solution.py:20
  29.7 0.5 collective-permute-start.7
  30.1 0.7 collective-permute-done.4.refs_1_
  30.9 0.0 collective-permute-start.8
  30.9 1.3 %collective-permute-done.5.refs_2_ = bf16[336,128]{1,0:T(8,128)(2,1)S(1)} collective-permute-done((bf16[336,128]{1,0:T(8,128)(2,1)S(1)}, bf16[336,128]{1,0:T(8,128)(2,1)S(1)}, u32[]{:S(2)}, u32[]{:S(2)}) %collective-permute-start.5) | collective-permute-done | bytes 86048 | tf_op jit(solution)/shard_map/ppermute | solution.py:20
  32.2 1.4 %collective-permute-start.9 = (bf16[336,128]{1,0:T(8,128)(2,1)S(1)}, bf16[336,128]{1,0:T(8,128)(2,1)S(1)}, u32[]{:S(2)}, u32[]{:S(2)}) collective-permute-start(bf16[336,128]{1,0:T(8,128)(2,1)S(1)} %get-tuple-element.31), channel_id=1, source_target_pairs={{0,6},{1,7},{2,0},{3,1},{4,2},{5,3},{6,4},{7,5},{8,14},{9,15},{10,... | collective-permute-start | bytes 258056 | tf_op jit(solution)/shard_map/ppermute | solution.py:20
  33.7 1.2 %collective-permute-done.6.refs_3_ = bf16[336,128]{1,0:T(8,128)(2,1)S(1)} collective-permute-done((bf16[336,128]{1,0:T(8,128)(2,1)S(1)}, bf16[336,128]{1,0:T(8,128)(2,1)S(1)}, u32[]{:S(2)}, u32[]{:S(2)}) %collective-permute-start.6) | collective-permute-done | bytes 86048 | tf_op jit(solution)/shard_map/ppermute | solution.py:20
  34.9 0.0 collective-permute-start.10
  34.9 0.5 collective-permute-done.7.refs_4_
  35.4 0.6 collective-permute-done.8.refs_5_
  36.1 0.9 %collective-permute-done.9.refs_6_ = bf16[336,128]{1,0:T(8,128)(2,1)S(1)} collective-permute-done((bf16[336,128]{1,0:T(8,128)(2,1)S(1)}, bf16[336,128]{1,0:T(8,128)(2,1)S(1)}, u32[]{:S(2)}, u32[]{:S(2)}) %collective-permute-start.9) | collective-permute-done | bytes 86048 | tf_op jit(solution)/shard_map/ppermute | solution.py:20
  36.9 0.1 collective-permute-done.10.refs_7_
  37.0 0.0 collective-permute-done.after_ref
  37.0 1.7 %place.1 = (f32[2,288,256]{2,1,0:T(8,128)S(1)}, bf16[2,160,256]{2,1,0:T(8,128)(2,1)S(1)}, bf16[2,160,256]{2,1,0:T(8,128)(2,1)S(1)}) custom-call(f32[2,128,256]{2,1,0:T(8,128)S(1)} %copy-done, f32[2,128,256]{2,1,0:T(8,128)S(1)} %collective-permute-done.after_ref, bf16[336,128]{1,0:T(8,128)(2,1)S(1)} %get-tuple-element.25.refs_0_, ...), custom_call_target="tpu_custom_call" | custom-call | tf_op jit(solution)/shard_map/place/pallas_call | solution.py:420
  38.7 1.1 %collective-permute-start.11 = (bf16[2,160,256]{2,1,0:T(8,128)(2,1)S(1)}, bf16[2,160,256]{2,1,0:T(8,128)(2,1)S(1)}, u32[]{:S(2)}, u32[]{:S(2)}) collective-permute-start(bf16[2,160,256]{2,1,0:T(8,128)(2,1)S(1)} %get-tuple-element.34), channel_id=1, source_target_pairs={{0,1},{1,2},{2,3},{3,4},{4,5},{5,6},{6,7},{7,0},{8,9},{9,10},{10,1... | collective-permute-start | bytes 491528 | tf_op jit(solution)/shard_map/ppermute | solution.py:20
  39.9 1.6 %collective-permute-start.12 = (bf16[2,160,256]{2,1,0:T(8,128)(2,1)S(1)}, bf16[2,160,256]{2,1,0:T(8,128)(2,1)S(1)}, u32[]{:S(2)}, u32[]{:S(2)}) collective-permute-start(bf16[2,160,256]{2,1,0:T(8,128)(2,1)S(1)} %get-tuple-element.35), channel_id=1, source_target_pairs={{0,7},{1,0},{2,1},{3,2},{4,3},{5,4},{6,5},{7,6},{8,15},{9,8},{10,9... | collective-permute-start | bytes 491528 | tf_op jit(solution)/shard_map/ppermute | solution.py:20
  41.5 0.0 copy-done.1
  41.5 1.3 %transfer.1.table_ref = bf16[2,9,256,256]{3,2,1,0:T(8,128)(2,1)S(1)} custom-call(f32[2]{0:T(128)S(1)} %copy-done.1), custom_call_target="tpu_custom_call" | custom-call | tf_op jit(solution)/shard_map/transfer/pallas_call | solution.py:475
  42.8 1.7 %collective-permute-done.11.above_ref = bf16[2,160,256]{2,1,0:T(8,128)(2,1)S(1)} collective-permute-done((bf16[2,160,256]{2,1,0:T(8,128)(2,1)S(1)}, bf16[2,160,256]{2,1,0:T(8,128)(2,1)S(1)}, u32[]{:S(2)}, u32[]{:S(2)}) %collective-permute-start.11) | collective-permute-done | bytes 163872 | tf_op jit(solution)/shard_map/ppermute | solution.py:20
  44.5 0.0 collective-permute-done.12.below_ref
  44.5 6.1 %filter_and_cut.1 = (f32[2,128,256]{2,1,0:T(8,128)}, bf16[4,8,64,128]{3,2,1,0:T(8,128)(2,1)S(1)}) custom-call(f32[2,288,256]{2,1,0:T(8,128)S(1)} %get-tuple-element.33.canvas_ref, bf16[2,160,256]{2,1,0:T(8,128)(2,1)S(1)} %collective-permute-done.11.above_ref, bf16[2,160,256]{2,1,0:T(8,128)(2,1)S(1)} %collective-permute-done.12.below_ref, ...), custom_call_target="tpu_custom_call" | custom-call | tf_op jit(solution)/shard_map/filter_and_cut/pallas_call | solution.py:633
  50.7 20.5 %all_to_all.5 = bf16[32,64,128]{2,1,0:T(8,128)(2,1)S(1)} all-to-all(bf16[32,64,128]{2,1,0:T(8,128)(2,1)S(1)} %bitcast.7), channel_id=1, replica_groups=mesh['tilt'=4,'tile'=8] {'tilt','tile'}, dimensions={0} | all-to-all | bytes 1048576 | tf_op jit(solution)/shard_map/all_to_all | solution.py:679
  71.1 8.5 %back_project.1 = f32[192,64,128]{2,1,0:T(8,128)} custom-call(f32[8]{0:T(128)} %angle_ref.5, bf16[4,512,128]{2,1,0:T(8,128)(2,1)S(1)} %bitcast.6, bf16[400,128]{1,0:T(8,128)(2,1)S(1)} %get-tuple-element.21.refs_0_, bf16[400,128]{1,0:T(8,128)(2,1)S(1)} %collective-permute-done.1.refs_1_, bf16[400,128]{1,0:T(8,128)(2,1)S(1)} %collective-permute-done.2.refs_2_, ...), custom_call_target="tpu_custom_call" | custom-call | tf_op jit(solution)/shard_map/back_project/pallas_call | solution.py:246
Async XLA Ops:
  0.6 15.5 %copy-start = (f32[2,128,256]{2,1,0:T(8,128)S(1)}, f32[2,128,256]{2,1,0:T(8,128)}, u32[]{:S(2)}) copy-start(f32[2,128,256]{2,1,0:T(8,128)} %measured_ref.3) | copy-start | bytes 786436
  6.5 35.0 %copy-start.1 = (f32[2]{0:T(128)S(1)}, f32[2]{0:T(128)}, u32[]{:S(2)}) copy-start(f32[2]{0:T(128)} %defocus_ref.1) | copy-start | bytes 28
  10.4 8.9 %collective-permute-start.3 = (bf16[400,128]{1,0:T(8,128)(2,1)S(1)}, bf16[400,128]{1,0:T(8,128)(2,1)S(1)}, u32[]{:S(2)}, u32[]{:S(2)}) collective-permute-start(bf16[400,128]{1,0:T(8,128)(2,1)S(1)} %get-tuple-element.24), channel_id=1, source_target_pairs={{0,24},{8,16},{16,8},{24,0},{1,25},{9,17},{17,9},{25,1},{2,26},{10... | collective-permute-start | bytes 307208 | tf_op jit(solution)/shard_map/ppermute | solution.py:26
  15.5 6.2 %collective-permute-start.1 = (bf16[400,128]{1,0:T(8,128)(2,1)S(1)}, bf16[400,128]{1,0:T(8,128)(2,1)S(1)}, u32[]{:S(2)}, u32[]{:S(2)}) collective-permute-start(bf16[400,128]{1,0:T(8,128)(2,1)S(1)} %get-tuple-element.22), channel_id=1, source_target_pairs={{0,8},{8,0},{16,24},{24,16},{1,9},{9,1},{17,25},{25,17},{2,10},{10... | collective-permute-start | bytes 307208 | tf_op jit(solution)/shard_map/ppermute | solution.py:26
  15.5 8.6 %collective-permute-start.2 = (bf16[400,128]{1,0:T(8,128)(2,1)S(1)}, bf16[400,128]{1,0:T(8,128)(2,1)S(1)}, u32[]{:S(2)}, u32[]{:S(2)}) collective-permute-start(bf16[400,128]{1,0:T(8,128)(2,1)S(1)} %get-tuple-element.23), channel_id=1, source_target_pairs={{0,16},{8,24},{16,0},{24,8},{1,17},{9,25},{17,1},{25,9},{2,18},{10... | collective-permute-start | bytes 307208 | tf_op jit(solution)/shard_map/ppermute | solution.py:26
  16.1 20.9 %collective-permute-start = (f32[2,128,256]{2,1,0:T(8,128)S(1)}, f32[2,128,256]{2,1,0:T(8,128)S(1)}, u32[]{:S(2)}, u32[]{:S(2)}) collective-permute-start(f32[2,128,256]{2,1,0:T(8,128)S(1)} %copy-done), channel_id=1, source_target_pairs={{0,7},{1,0},{2,1},{3,2},{4,3},{5,4},{6,5},{7,6},{8,15},{9,8},{10,9... | collective-permute-start | bytes 786440 | tf_op jit(solution)/shard_map/ppermute | solution.py:20
  25.7 5.2 %collective-permute-start.4 = (bf16[336,128]{1,0:T(8,128)(2,1)S(1)}, bf16[336,128]{1,0:T(8,128)(2,1)S(1)}, u32[]{:S(2)}, u32[]{:S(2)}) collective-permute-start(bf16[336,128]{1,0:T(8,128)(2,1)S(1)} %get-tuple-element.26), channel_id=1, source_target_pairs={{0,1},{1,2},{2,3},{3,4},{4,5},{5,6},{6,7},{7,0},{8,9},{9,10},{10,1... | collective-permute-start | bytes 258056 | tf_op jit(solution)/shard_map/ppermute | solution.py:20
  25.8 6.5 %collective-permute-start.5 = (bf16[336,128]{1,0:T(8,128)(2,1)S(1)}, bf16[336,128]{1,0:T(8,128)(2,1)S(1)}, u32[]{:S(2)}, u32[]{:S(2)}) collective-permute-start(bf16[336,128]{1,0:T(8,128)(2,1)S(1)} %get-tuple-element.27), channel_id=1, source_target_pairs={{0,2},{1,3},{2,4},{3,5},{4,6},{5,7},{6,0},{7,1},{8,10},{9,11},{10,... | collective-permute-start | bytes 258056 | tf_op jit(solution)/shard_map/ppermute | solution.py:20
  27.3 7.6 %collective-permute-start.6 = (bf16[336,128]{1,0:T(8,128)(2,1)S(1)}, bf16[336,128]{1,0:T(8,128)(2,1)S(1)}, u32[]{:S(2)}, u32[]{:S(2)}) collective-permute-start(bf16[336,128]{1,0:T(8,128)(2,1)S(1)} %get-tuple-element.28), channel_id=1, source_target_pairs={{0,3},{1,4},{2,5},{3,6},{4,7},{5,0},{6,1},{7,2},{8,11},{9,12},{10,... | collective-permute-start | bytes 258056 | tf_op jit(solution)/shard_map/ppermute | solution.py:20
  29.7 5.8 %collective-permute-start.7 = (bf16[336,128]{1,0:T(8,128)(2,1)S(1)}, bf16[336,128]{1,0:T(8,128)(2,1)S(1)}, u32[]{:S(2)}, u32[]{:S(2)}) collective-permute-start(bf16[336,128]{1,0:T(8,128)(2,1)S(1)} %get-tuple-element.29), channel_id=1, source_target_pairs={{0,4},{1,5},{2,6},{3,7},{4,0},{5,1},{6,2},{7,3},{8,12},{9,13},{10,... | collective-permute-start | bytes 258056 | tf_op jit(solution)/shard_map/ppermute | solution.py:20
  30.9 5.2 %collective-permute-start.8 = (bf16[336,128]{1,0:T(8,128)(2,1)S(1)}, bf16[336,128]{1,0:T(8,128)(2,1)S(1)}, u32[]{:S(2)}, u32[]{:S(2)}) collective-permute-start(bf16[336,128]{1,0:T(8,128)(2,1)S(1)} %get-tuple-element.30), channel_id=1, source_target_pairs={{0,5},{1,6},{2,7},{3,0},{4,1},{5,2},{6,3},{7,4},{8,13},{9,14},{10,... | collective-permute-start | bytes 258056 | tf_op jit(solution)/shard_map/ppermute | solution.py:20
  32.2 4.7 %collective-permute-start.9 = (bf16[336,128]{1,0:T(8,128)(2,1)S(1)}, bf16[336,128]{1,0:T(8,128)(2,1)S(1)}, u32[]{:S(2)}, u32[]{:S(2)}) collective-permute-start(bf16[336,128]{1,0:T(8,128)(2,1)S(1)} %get-tuple-element.31), channel_id=1, source_target_pairs={{0,6},{1,7},{2,0},{3,1},{4,2},{5,3},{6,4},{7,5},{8,14},{9,15},{10,... | collective-permute-start | bytes 258056 | tf_op jit(solution)/shard_map/ppermute | solution.py:20
  34.9 2.1 %collective-permute-start.10 = (bf16[336,128]{1,0:T(8,128)(2,1)S(1)}, bf16[336,128]{1,0:T(8,128)(2,1)S(1)}, u32[]{:S(2)}, u32[]{:S(2)}) collective-permute-start(bf16[336,128]{1,0:T(8,128)(2,1)S(1)} %get-tuple-element.32), channel_id=1, source_target_pairs={{0,7},{1,0},{2,1},{3,2},{4,3},{5,4},{6,5},{7,6},{8,15},{9,8},{10,9... | collective-permute-start | bytes 258056 | tf_op jit(solution)/shard_map/ppermute | solution.py:20
  38.7 5.8 %collective-permute-start.11 = (bf16[2,160,256]{2,1,0:T(8,128)(2,1)S(1)}, bf16[2,160,256]{2,1,0:T(8,128)(2,1)S(1)}, u32[]{:S(2)}, u32[]{:S(2)}) collective-permute-start(bf16[2,160,256]{2,1,0:T(8,128)(2,1)S(1)} %get-tuple-element.34), channel_id=1, source_target_pairs={{0,1},{1,2},{2,3},{3,4},{4,5},{5,6},{6,7},{7,0},{8,9},{9,10},{10,1... | collective-permute-start | bytes 491528 | tf_op jit(solution)/shard_map/ppermute | solution.py:20
  39.9 4.7 %collective-permute-start.12 = (bf16[2,160,256]{2,1,0:T(8,128)(2,1)S(1)}, bf16[2,160,256]{2,1,0:T(8,128)(2,1)S(1)}, u32[]{:S(2)}, u32[]{:S(2)}) collective-permute-start(bf16[2,160,256]{2,1,0:T(8,128)(2,1)S(1)} %get-tuple-element.35), channel_id=1, source_target_pairs={{0,7},{1,0},{2,1},{3,2},{4,3},{5,4},{6,5},{7,6},{8,15},{9,8},{10,9... | collective-permute-start | bytes 491528 | tf_op jit(solution)/shard_map/ppermute | solution.py:20

commit v3 on v1

--- a/solution.py
+++ b/solution.py
@@ -293,7 +293,7 @@
 
     for d in range(tile_count):
         out = outs[d]
-        strip = my_tile ^ d
+        strip = lax.rem(my_tile + d, tile_count)
         metas = []
 
         def item_at(offset, r):
@@ -542,7 +542,7 @@
     column = iota_apart((image_width, width), 0, 1)
     meta = capacity * (height + 2 * REACH)
     for d, parcel in enumerate(parcels):
-        sender = my_tile ^ d
+        sender = lax.rem(my_tile + tile_count - d, tile_count)
         for r in range(capacity):
             top = parcel[meta + 2 * r : meta + 2 * r + 1, :].astype(F32)
             picks = []
@@ -596,16 +596,18 @@
     slabs = [None] * groups
     volume = far(volumes.reshape(rows, depth, width))
     half = groups // 2 + 1
-    early, late = tuple(range(1, half)), (*range(half, groups), 0)
+    early, middle = tuple(range(1, half)), tuple(range(half, groups))
     sizes = (depth, width, strip_rows, capacity)
     *parts, flat = project(volume, rows_of, angles, tilts, groups, early, True, *sizes)
     for k, part in zip(early, parts, strict=True):
         slabs[k] = swap(part, "tilt", k)
-    parts = project(flat, rows_of, angles, tilts, groups, late, False, *sizes)
-    for k, part in zip(late, parts, strict=True):
-        slabs[k] = swap(part, "tilt", k) if k else part
+    if middle:
+        parts = project(flat, rows_of, angles, tilts, groups, middle, False, *sizes)
+        for k, part in zip(middle, parts, strict=True):
+            slabs[k] = swap(part, "tilt", k)
+    (slabs[0],) = project(flat, rows_of, angles, tilts, groups, (0,), False, *sizes)
     parcels = pack(slabs, rows_of, cols_of, slab_rows, tile_count, strip_rows, capacity)
-    parcels = [p if d == 0 else swap(p, "tile", d) for d, p in enumerate(parcels)]
+    parcels = [p if d == 0 else ring(p, "tile", d) for d, p in enumerate(parcels)]
     canvas, onward, backward = place(measured, after, parcels, height, capacity)
     above, below = ring(onward, "tile", 1), ring(backward, "tile", -1)
     residual, cuts = filter_and_cut(

time: 80.7 us -> 78.6 us (0.974)
  waiting for transfers between devices: 14.7 us -> 10.8 us
  Pallas kernels: 28.5 us -> 30.6 us
  starting transfers between devices: 17 us -> 15.7 us
  blocking collectives: 19.6 us -> 20.5 us
    ppermute x10 -> x3, waiting for transfers between devices: 12.3 us -> 3.69 us  [swap(): return lax.ppermute(block, axis, [(i, i ^ distance) for i in range(count)])]
    ppermute x10 -> x3, starting transfers between devices: 13 us -> 5.79 us  [swap(): return lax.ppermute(block, axis, [(i, i ^ distance) for i in range(count)])]
    ppermute x3 -> x10, starting transfers between devices: 3.99 us -> 9.95 us  [ring(): lax.ppermute(block, axis, [(i, (i + distance) % count) for i in range(cou...]
    ppermute x3 -> x10, waiting for transfers between devices: 2.42 us -> 7.14 us  [ring(): lax.ppermute(block, axis, [(i, (i + distance) % count) for i in range(cou...]
    pallas_call x2 -> x3, Pallas kernels: 9.72 us -> 11.8 us  [project(): pl.pallas_call(functools.partial(project_kernel, depth=depth, tilts=tilts...]
    all_to_all x1, blocking collectives: 19.6 us -> 20.5 us  [shards(): lax.all_to_all(cuts, ('tilt', 'tile'), split_axis=0, concat_axis=0, tiled...]
  transfers between devices with their start and end apart: 13 -> 13, of which waited for: 8 -> 10; matrix products, arithmetic and copies ran while one was open for 0% -> 0% of each run, Pallas kernels for 4% -> 7%
where the time goes in v3:
time: 78.6 us; the launch traced here: 78.4 us
  Pallas kernels  30.6 us (39%)
  blocking collectives  20.5 us (26%)
  starting transfers between devices  15.7 us (20%)
  waiting for transfers between devices  10.8 us (14%)
    all_to_all x1, blocking collectives, shards(): lax.all_to_all(cuts, ('tilt', 'tile'), split_axis=0, concat_axis=0, tiled...  20.5 us
    pallas_call x3, Pallas kernels, project(): pl.pallas_call(functools.partial(project_kernel, depth=depth, tilts=tilts...  11.8 us
    ppermute x10, starting transfers between devices, ring(): lax.ppermute(block, axis, [(i, (i + distance) % count) for i in range(cou...  9.95 us
    pallas_call x1, Pallas kernels, back_project(): pl.pallas_call(functools.partial(back_kernel, depth=depth, tilts=tilts, b...  8.51 us
    ppermute x10, waiting for transfers between devices, ring(): lax.ppermute(block, axis, [(i, (i + distance) % count) for i in range(cou...  7.14 us
    ppermute x3, starting transfers between devices, swap(): return lax.ppermute(block, axis, [(i, i ^ distance) for i in range(count)])  5.79 us
    pallas_call x1, Pallas kernels, filter_and_cut(): pl.pallas_call(functools.partial(filter_kernel, height=height, capacity=c...  5.7 us
    ppermute x3, waiting for transfers between devices, swap(): return lax.ppermute(block, axis, [(i, i ^ distance) for i in range(count)])  3.69 us
  transfers between devices with their start and end apart: 13, of which 10 were waited for; matrix products, arithmetic and copies ran while one was open for 0% of the time, Pallas kernels for 7%

profile of v3, /device:TPU:0, one launch (start us, length us, event | category | flops | bytes accessed | tf_op | source)
XLA Modules:
  0.0 78.4 jit_solution(4075862920986825400)
XLA Ops:
  0.6 0.0 copy-start
  0.6 5.9 %project_first.1 = (bf16[400,128]{1,0:T(8,128)(2,1)S(1)}, bf16[400,128]{1,0:T(8,128)(2,1)S(1)}, bf16[192,8192]{1,0:T(8,128)(2,1)S(1)}) custom-call(s32[2,6]{1,0:T(2,128)} %bitcast.10, f32[8]{0:T(128)} %angle_ref.7, bf16[192,64,128]{2,1,0:T(8,128)(2,1)} %bitcast.9), custom_call_target="tpu_custom_call" | custom-call | tf_op jit(solution)/shard_map/project_first/pallas_call | solution.py:165
  6.5 3.0 %project_rest.3 = bf16[400,128]{1,0:T(8,128)(2,1)S(1)} custom-call(s32[2,6]{1,0:T(2,128)} %bitcast.11, f32[8]{0:T(128)} %angle_ref.7, bf16[192,8192]{1,0:T(8,128)(2,1)S(1)} %get-tuple-element.18.vol_ref), custom_call_target="tpu_custom_call" | custom-call | tf_op jit(solution)/shard_map/project_rest/pallas_call | solution.py:165
  9.5 0.0 copy-start.1
  9.5 5.1 %collective-permute-start.3 = (bf16[400,128]{1,0:T(8,128)(2,1)S(1)}, bf16[400,128]{1,0:T(8,128)(2,1)S(1)}, u32[]{:S(2)}, u32[]{:S(2)}) collective-permute-start(bf16[400,128]{1,0:T(8,128)(2,1)S(1)} %project_rest.3), channel_id=1, source_target_pairs={{0,24},{8,16},{16,8},{24,0},{1,25},{9,17},{17,9},{25,1},{2,26},{10... | collective-permute-start | bytes 307208 | tf_op jit(solution)/shard_map/ppermute | solution.py:26
  14.6 0.0 collective-permute-start.1
  14.6 0.6 collective-permute-start.2
  15.3 0.0 copy-done
  15.3 1.3 %collective-permute-start = (f32[2,128,256]{2,1,0:T(8,128)S(1)}, f32[2,128,256]{2,1,0:T(8,128)S(1)}, u32[]{:S(2)}, u32[]{:S(2)}) collective-permute-start(f32[2,128,256]{2,1,0:T(8,128)S(1)} %copy-done), channel_id=1, source_target_pairs={{0,7},{1,0},{2,1},{3,2},{4,3},{5,4},{6,5},{7,6},{8,15},{9,8},{10,9... | collective-permute-start | bytes 786440 | tf_op jit(solution)/shard_map/ppermute | solution.py:20
  16.6 2.9 %project_rest.2.refs_0_ = bf16[400,128]{1,0:T(8,128)(2,1)S(1)} custom-call(s32[2,6]{1,0:T(2,128)} %bitcast.12, f32[8]{0:T(128)} %angle_ref.7, bf16[192,8192]{1,0:T(8,128)(2,1)S(1)} %get-tuple-element.18.vol_ref), custom_call_target="tpu_custom_call" | custom-call | tf_op jit(solution)/shard_map/project_rest/pallas_call | solution.py:165
  19.5 0.0 collective-permute-done.3.refs_3_
  19.6 1.2 %collective-permute-done.1.refs_1_ = bf16[400,128]{1,0:T(8,128)(2,1)S(1)} collective-permute-done((bf16[400,128]{1,0:T(8,128)(2,1)S(1)}, bf16[400,128]{1,0:T(8,128)(2,1)S(1)}, u32[]{:S(2)}, u32[]{:S(2)}) %collective-permute-start.1) | collective-permute-done | bytes 102432 | tf_op jit(solution)/shard_map/ppermute | solution.py:26
  20.8 2.5 %collective-permute-done.2.refs_2_ = bf16[400,128]{1,0:T(8,128)(2,1)S(1)} collective-permute-done((bf16[400,128]{1,0:T(8,128)(2,1)S(1)}, bf16[400,128]{1,0:T(8,128)(2,1)S(1)}, u32[]{:S(2)}, u32[]{:S(2)}) %collective-permute-start.2) | collective-permute-done | bytes 102432 | tf_op jit(solution)/shard_map/ppermute | solution.py:26
  23.2 1.6 %pack.1 = (bf16[336,128]{1,0:T(8,128)(2,1)S(1)}, bf16[336,128]{1,0:T(8,128)(2,1)S(1)}, bf16[336,128]{1,0:T(8,128)(2,1)S(1)}, bf16[336,128]{1,0:T(8,128)(2,1)S(1)...) custom-call(s32[2,6]{1,0:T(2,128)} %bitcast.13, ...), custom_call_target="tpu_custom_call" | custom-call | tf_op jit(solution)/shard_map/pack/pallas_call | solution.py:328
  24.8 0.1 collective-permute-start.4
  24.9 1.5 %collective-permute-start.5 = (bf16[336,128]{1,0:T(8,128)(2,1)S(1)}, bf16[336,128]{1,0:T(8,128)(2,1)S(1)}, u32[]{:S(2)}, u32[]{:S(2)}) collective-permute-start(bf16[336,128]{1,0:T(8,128)(2,1)S(1)} %get-tuple-element.23), channel_id=1, source_target_pairs={{0,2},{1,3},{2,4},{3,5},{4,6},{5,7},{6,0},{7,1},{8,10},{9,11},{10,... | collective-permute-start | bytes 258056 | tf_op jit(solution)/shard_map/ppermute | solution.py:20
  26.4 2.4 %collective-permute-start.6 = (bf16[336,128]{1,0:T(8,128)(2,1)S(1)}, bf16[336,128]{1,0:T(8,128)(2,1)S(1)}, u32[]{:S(2)}, u32[]{:S(2)}) collective-permute-start(bf16[336,128]{1,0:T(8,128)(2,1)S(1)} %get-tuple-element.24), channel_id=1, source_target_pairs={{0,3},{1,4},{2,5},{3,6},{4,7},{5,0},{6,1},{7,2},{8,11},{9,12},{10,... | collective-permute-start | bytes 258056 | tf_op jit(solution)/shard_map/ppermute | solution.py:20
  28.8 0.5 collective-permute-start.7
  29.3 0.7 collective-permute-done.4.refs_1_
  30.0 0.0 collective-permute-start.8
  30.0 1.3 %collective-permute-done.5.refs_2_ = bf16[336,128]{1,0:T(8,128)(2,1)S(1)} collective-permute-done((bf16[336,128]{1,0:T(8,128)(2,1)S(1)}, bf16[336,128]{1,0:T(8,128)(2,1)S(1)}, u32[]{:S(2)}, u32[]{:S(2)}) %collective-permute-start.5) | collective-permute-done | bytes 86048 | tf_op jit(solution)/shard_map/ppermute | solution.py:20
  31.3 1.4 %collective-permute-start.9 = (bf16[336,128]{1,0:T(8,128)(2,1)S(1)}, bf16[336,128]{1,0:T(8,128)(2,1)S(1)}, u32[]{:S(2)}, u32[]{:S(2)}) collective-permute-start(bf16[336,128]{1,0:T(8,128)(2,1)S(1)} %get-tuple-element.27), channel_id=1, source_target_pairs={{0,6},{1,7},{2,0},{3,1},{4,2},{5,3},{6,4},{7,5},{8,14},{9,15},{10,... | collective-permute-start | bytes 258056 | tf_op jit(solution)/shard_map/ppermute | solution.py:20
  32.8 1.3 %collective-permute-done.6.refs_3_ = bf16[336,128]{1,0:T(8,128)(2,1)S(1)} collective-permute-done((bf16[336,128]{1,0:T(8,128)(2,1)S(1)}, bf16[336,128]{1,0:T(8,128)(2,1)S(1)}, u32[]{:S(2)}, u32[]{:S(2)}) %collective-permute-start.6) | collective-permute-done | bytes 86048 | tf_op jit(solution)/shard_map/ppermute | solution.py:20
  34.1 0.0 collective-permute-start.10
  34.1 0.5 collective-permute-done.7.refs_4_
  34.5 0.7 collective-permute-done.8.refs_5_
  35.2 0.9 %collective-permute-done.9.refs_6_ = bf16[336,128]{1,0:T(8,128)(2,1)S(1)} collective-permute-done((bf16[336,128]{1,0:T(8,128)(2,1)S(1)}, bf16[336,128]{1,0:T(8,128)(2,1)S(1)}, u32[]{:S(2)}, u32[]{:S(2)}) %collective-permute-start.9) | collective-permute-done | bytes 86048 | tf_op jit(solution)/shard_map/ppermute | solution.py:20
  36.1 0.1 collective-permute-done.10.refs_7_
  36.2 0.0 collective-permute-done.after_ref
  36.2 1.7 %place.1 = (f32[2,288,256]{2,1,0:T(8,128)S(1)}, bf16[2,160,256]{2,1,0:T(8,128)(2,1)S(1)}, bf16[2,160,256]{2,1,0:T(8,128)(2,1)S(1)}) custom-call(f32[2,128,256]{2,1,0:T(8,128)S(1)} %copy-done, f32[2,128,256]{2,1,0:T(8,128)S(1)} %collective-permute-done.after_ref, bf16[336,128]{1,0:T(8,128)(2,1)S(1)} %get-tuple-element.21.refs_0_, ...), custom_call_target="tpu_custom_call" | custom-call | tf_op jit(solution)/shard_map/place/pallas_call | solution.py:420
  37.9 1.1 %collective-permute-start.11 = (bf16[2,160,256]{2,1,0:T(8,128)(2,1)S(1)}, bf16[2,160,256]{2,1,0:T(8,128)(2,1)S(1)}, u32[]{:S(2)}, u32[]{:S(2)}) collective-permute-start(bf16[2,160,256]{2,1,0:T(8,128)(2,1)S(1)} %get-tuple-element.30), channel_id=1, source_target_pairs={{0,1},{1,2},{2,3},{3,4},{4,5},{5,6},{6,7},{7,0},{8,9},{9,10},{10,1... | collective-permute-start | bytes 491528 | tf_op jit(solution)/shard_map/ppermute | solution.py:20
  39.0 1.6 %collective-permute-start.12 = (bf16[2,160,256]{2,1,0:T(8,128)(2,1)S(1)}, bf16[2,160,256]{2,1,0:T(8,128)(2,1)S(1)}, u32[]{:S(2)}, u32[]{:S(2)}) collective-permute-start(bf16[2,160,256]{2,1,0:T(8,128)(2,1)S(1)} %get-tuple-element.31), channel_id=1, source_target_pairs={{0,7},{1,0},{2,1},{3,2},{4,3},{5,4},{6,5},{7,6},{8,15},{9,8},{10,9... | collective-permute-start | bytes 491528 | tf_op jit(solution)/shard_map/ppermute | solution.py:20
  40.6 0.0 copy-done.1
  40.6 1.3 %transfer.1.table_ref = bf16[2,9,256,256]{3,2,1,0:T(8,128)(2,1)S(1)} custom-call(f32[2]{0:T(128)S(1)} %copy-done.1), custom_call_target="tpu_custom_call" | custom-call | tf_op jit(solution)/shard_map/transfer/pallas_call | solution.py:475
  41.9 1.7 %collective-permute-done.11.above_ref = bf16[2,160,256]{2,1,0:T(8,128)(2,1)S(1)} collective-permute-done((bf16[2,160,256]{2,1,0:T(8,128)(2,1)S(1)}, bf16[2,160,256]{2,1,0:T(8,128)(2,1)S(1)}, u32[]{:S(2)}, u32[]{:S(2)}) %collective-permute-start.11) | collective-permute-done | bytes 163872 | tf_op jit(solution)/shard_map/ppermute | solution.py:20
  43.7 0.0 collective-permute-done.12.below_ref
  43.7 5.7 %filter_and_cut.1 = (f32[2,128,256]{2,1,0:T(8,128)}, bf16[4,8,64,128]{3,2,1,0:T(8,128)(2,1)S(1)}) custom-call(f32[2,288,256]{2,1,0:T(8,128)S(1)} %get-tuple-element.29.canvas_ref, bf16[2,160,256]{2,1,0:T(8,128)(2,1)S(1)} %collective-permute-done.11.above_ref, bf16[2,160,256]{2,1,0:T(8,128)(2,1)S(1)} %collective-permute-done.12.below_ref, ...), custom_call_target="tpu_custom_call" | custom-call | tf_op jit(solution)/shard_map/filter_and_cut/pallas_call | solution.py:572
  49.4 20.5 %all_to_all.5 = bf16[32,64,128]{2,1,0:T(8,128)(2,1)S(1)} all-to-all(bf16[32,64,128]{2,1,0:T(8,128)(2,1)S(1)} %bitcast.7), channel_id=1, replica_groups=mesh['tilt'=4,'tile'=8] {'tilt','tile'}, dimensions={0} | all-to-all | bytes 1048576 | tf_op jit(solution)/shard_map/all_to_all | solution.py:617
  69.8 8.5 %back_project.1 = f32[192,64,128]{2,1,0:T(8,128)} custom-call(f32[8]{0:T(128)} %angle_ref.7, bf16[4,512,128]{2,1,0:T(8,128)(2,1)S(1)} %bitcast.6, bf16[400,128]{1,0:T(8,128)(2,1)S(1)} %project_rest.2.refs_0_, bf16[400,128]{1,0:T(8,128)(2,1)S(1)} %collective-permute-done.1.refs_1_, bf16[400,128]{1,0:T(8,128)(2,1)S(1)} %collective-permute-done.2.refs_2_, ...), custom_call_target="tpu_custom_call" | custom-call | tf_op jit(solution)/shard_map/back_project/pallas_call | solution.py:246
Async XLA Ops:
  0.6 14.6 %copy-start = (f32[2,128,256]{2,1,0:T(8,128)S(1)}, f32[2,128,256]{2,1,0:T(8,128)}, u32[]{:S(2)}) copy-start(f32[2,128,256]{2,1,0:T(8,128)} %measured_ref.3) | copy-start | bytes 786436
  9.5 31.1 %copy-start.1 = (f32[2]{0:T(128)S(1)}, f32[2]{0:T(128)}, u32[]{:S(2)}) copy-start(f32[2]{0:T(128)} %defocus_ref.1) | copy-start | bytes 28
  9.5 10.1 %collective-permute-start.3 = (bf16[400,128]{1,0:T(8,128)(2,1)S(1)}, bf16[400,128]{1,0:T(8,128)(2,1)S(1)}, u32[]{:S(2)}, u32[]{:S(2)}) collective-permute-start(bf16[400,128]{1,0:T(8,128)(2,1)S(1)} %project_rest.3), channel_id=1, source_target_pairs={{0,24},{8,16},{16,8},{24,0},{1,25},{9,17},{17,9},{25,1},{2,26},{10... | collective-permute-start | bytes 307208 | tf_op jit(solution)/shard_map/ppermute | solution.py:26
  14.6 6.1 %collective-permute-start.1 = (bf16[400,128]{1,0:T(8,128)(2,1)S(1)}, bf16[400,128]{1,0:T(8,128)(2,1)S(1)}, u32[]{:S(2)}, u32[]{:S(2)}) collective-permute-start(bf16[400,128]{1,0:T(8,128)(2,1)S(1)} %get-tuple-element.19), channel_id=1, source_target_pairs={{0,8},{8,0},{16,24},{24,16},{1,9},{9,1},{17,25},{25,17},{2,10},{10... | collective-permute-start | bytes 307208 | tf_op jit(solution)/shard_map/ppermute | solution.py:26
  14.6 8.6 %collective-permute-start.2 = (bf16[400,128]{1,0:T(8,128)(2,1)S(1)}, bf16[400,128]{1,0:T(8,128)(2,1)S(1)}, u32[]{:S(2)}, u32[]{:S(2)}) collective-permute-start(bf16[400,128]{1,0:T(8,128)(2,1)S(1)} %get-tuple-element.20), channel_id=1, source_target_pairs={{0,16},{8,24},{16,0},{24,8},{1,17},{9,25},{17,1},{25,9},{2,18},{10... | collective-permute-start | bytes 307208 | tf_op jit(solution)/shard_map/ppermute | solution.py:26
  15.3 20.9 %collective-permute-start = (f32[2,128,256]{2,1,0:T(8,128)S(1)}, f32[2,128,256]{2,1,0:T(8,128)S(1)}, u32[]{:S(2)}, u32[]{:S(2)}) collective-permute-start(f32[2,128,256]{2,1,0:T(8,128)S(1)} %copy-done), channel_id=1, source_target_pairs={{0,7},{1,0},{2,1},{3,2},{4,3},{5,4},{6,5},{7,6},{8,15},{9,8},{10,9... | collective-permute-start | bytes 786440 | tf_op jit(solution)/shard_map/ppermute | solution.py:20
  24.8 5.2 %collective-permute-start.4 = (bf16[336,128]{1,0:T(8,128)(2,1)S(1)}, bf16[336,128]{1,0:T(8,128)(2,1)S(1)}, u32[]{:S(2)}, u32[]{:S(2)}) collective-permute-start(bf16[336,128]{1,0:T(8,128)(2,1)S(1)} %get-tuple-element.22), channel_id=1, source_target_pairs={{0,1},{1,2},{2,3},{3,4},{4,5},{5,6},{6,7},{7,0},{8,9},{9,10},{10,1... | collective-permute-start | bytes 258056 | tf_op jit(solution)/shard_map/ppermute | solution.py:20
  24.9 6.5 %collective-permute-start.5 = (bf16[336,128]{1,0:T(8,128)(2,1)S(1)}, bf16[336,128]{1,0:T(8,128)(2,1)S(1)}, u32[]{:S(2)}, u32[]{:S(2)}) collective-permute-start(bf16[336,128]{1,0:T(8,128)(2,1)S(1)} %get-tuple-element.23), channel_id=1, source_target_pairs={{0,2},{1,3},{2,4},{3,5},{4,6},{5,7},{6,0},{7,1},{8,10},{9,11},{10,... | collective-permute-start | bytes 258056 | tf_op jit(solution)/shard_map/ppermute | solution.py:20
  26.4 7.6 %collective-permute-start.6 = (bf16[336,128]{1,0:T(8,128)(2,1)S(1)}, bf16[336,128]{1,0:T(8,128)(2,1)S(1)}, u32[]{:S(2)}, u32[]{:S(2)}) collective-permute-start(bf16[336,128]{1,0:T(8,128)(2,1)S(1)} %get-tuple-element.24), channel_id=1, source_target_pairs={{0,3},{1,4},{2,5},{3,6},{4,7},{5,0},{6,1},{7,2},{8,11},{9,12},{10,... | collective-permute-start | bytes 258056 | tf_op jit(solution)/shard_map/ppermute | solution.py:20
  28.8 5.7 %collective-permute-start.7 = (bf16[336,128]{1,0:T(8,128)(2,1)S(1)}, bf16[336,128]{1,0:T(8,128)(2,1)S(1)}, u32[]{:S(2)}, u32[]{:S(2)}) collective-permute-start(bf16[336,128]{1,0:T(8,128)(2,1)S(1)} %get-tuple-element.25), channel_id=1, source_target_pairs={{0,4},{1,5},{2,6},{3,7},{4,0},{5,1},{6,2},{7,3},{8,12},{9,13},{10,... | collective-permute-start | bytes 258056 | tf_op jit(solution)/shard_map/ppermute | solution.py:20
  30.0 5.1 %collective-permute-start.8 = (bf16[336,128]{1,0:T(8,128)(2,1)S(1)}, bf16[336,128]{1,0:T(8,128)(2,1)S(1)}, u32[]{:S(2)}, u32[]{:S(2)}) collective-permute-start(bf16[336,128]{1,0:T(8,128)(2,1)S(1)} %get-tuple-element.26), channel_id=1, source_target_pairs={{0,5},{1,6},{2,7},{3,0},{4,1},{5,2},{6,3},{7,4},{8,13},{9,14},{10,... | collective-permute-start | bytes 258056 | tf_op jit(solution)/shard_map/ppermute | solution.py:20
  31.3 4.7 %collective-permute-start.9 = (bf16[336,128]{1,0:T(8,128)(2,1)S(1)}, bf16[336,128]{1,0:T(8,128)(2,1)S(1)}, u32[]{:S(2)}, u32[]{:S(2)}) collective-permute-start(bf16[336,128]{1,0:T(8,128)(2,1)S(1)} %get-tuple-element.27), channel_id=1, source_target_pairs={{0,6},{1,7},{2,0},{3,1},{4,2},{5,3},{6,4},{7,5},{8,14},{9,15},{10,... | collective-permute-start | bytes 258056 | tf_op jit(solution)/shard_map/ppermute | solution.py:20
  34.1 2.1 %collective-permute-start.10 = (bf16[336,128]{1,0:T(8,128)(2,1)S(1)}, bf16[336,128]{1,0:T(8,128)(2,1)S(1)}, u32[]{:S(2)}, u32[]{:S(2)}) collective-permute-start(bf16[336,128]{1,0:T(8,128)(2,1)S(1)} %get-tuple-element.28), channel_id=1, source_target_pairs={{0,7},{1,0},{2,1},{3,2},{4,3},{5,4},{6,5},{7,6},{8,15},{9,8},{10,9... | collective-permute-start | bytes 258056 | tf_op jit(solution)/shard_map/ppermute | solution.py:20
  37.9 5.8 %collective-permute-start.11 = (bf16[2,160,256]{2,1,0:T(8,128)(2,1)S(1)}, bf16[2,160,256]{2,1,0:T(8,128)(2,1)S(1)}, u32[]{:S(2)}, u32[]{:S(2)}) collective-permute-start(bf16[2,160,256]{2,1,0:T(8,128)(2,1)S(1)} %get-tuple-element.30), channel_id=1, source_target_pairs={{0,1},{1,2},{2,3},{3,4},{4,5},{5,6},{6,7},{7,0},{8,9},{9,10},{10,1... | collective-permute-start | bytes 491528 | tf_op jit(solution)/shard_map/ppermute | solution.py:20
  39.0 4.7 %collective-permute-start.12 = (bf16[2,160,256]{2,1,0:T(8,128)(2,1)S(1)}, bf16[2,160,256]{2,1,0:T(8,128)(2,1)S(1)}, u32[]{:S(2)}, u32[]{:S(2)}) collective-permute-start(bf16[2,160,256]{2,1,0:T(8,128)(2,1)S(1)} %get-tuple-element.31), channel_id=1, source_target_pairs={{0,7},{1,0},{2,1},{3,2},{4,3},{5,4},{6,5},{7,6},{8,15},{9,8},{10,9... | collective-permute-start | bytes 491528 | tf_op jit(solution)/shard_map/ppermute | solution.py:20

commit v4 on v3

--- a/solution.py
+++ b/solution.py
@@ -92,41 +92,13 @@
     return block.astype(BF)
 
 
-def project_kernel(
-    row_ref, angle_ref, vol_ref, *refs, depth, tilts, groups, ks, first, strip_rows, capacity
-):
-    outs, (total, sines) = refs[: len(ks)], refs[-2:]
-    step = pl.program_id(0)
+def add_products(step, pair_at, total, sines, ks, tilts, layers, depth):
+    width = sines.shape[2]
     me = lax.axis_index("tilt")
-    if first:
-        lhs, wide = refs[len(ks)], refs[len(ks) + 1]
-        rows, layers, width = vol_ref.shape
-        wide[...] = vol_ref[...].reshape(rows * layers, width).astype(F32)
-
-        def pair_at(z):
-            pair = [wide[pl.ds(z + h, rows, stride=layers), :].astype(BF) for h in range(2)]
-            pair = jnp.concatenate(pair, axis=1)
-            lhs[:, z * width : (z + 2) * width] = pair
-            return pair
-    else:
-        lhs = vol_ref
-        rows = lhs.shape[0]
-        width = outs[0].shape[1]
-        layers = lhs.shape[1] // width
-
-        def pair_at(z):
-            return lhs[:, z * width : (z + 2) * width]
-
-    @pl.when(step == 0)
-    def _():
-        total[...] = jnp.zeros_like(total)
-        note_sines(angle_ref, sines)
-
     apart = iota_apart((width, width), 1, 0)
 
     def block(k, z, t):
-        sine = sines[(me ^ k) * tilts + t]
-        return tap_block(apart, sine, step * layers + z, depth)
+        return tap_block(apart, sines[(me ^ k) * tilts + t], step * layers + z, depth)
 
     following = pair_at(0)
     for z in range(0, layers, 2):
@@ -144,15 +116,62 @@
             span = slice(i * tilts * width, (i + 1) * tilts * width)
             total[:, span] += jnp.dot(pair, table, preferred_element_type=F32)
 
+
+def write_slabs(row_ref, total, outs, tilts, strip_rows, capacity):
+    rows, width = total.shape[0], outs[0].shape[1]
+    _, slots = slots_of_items(row_ref, strip_rows, capacity)
+    meta = splat_rows(slots, outs[0].shape[0] - tilts * rows, width)
+    for i, out in enumerate(outs):
+        for t in range(tilts):
+            start = (i * tilts + t) * width
+            out[t * rows : (t + 1) * rows, :] = total[:, start : start + width].astype(BF)
+        out[tilts * rows :, :] = meta
+
+
+def project_first_kernel(
+    row_ref, angle_ref, vol_ref, *refs, depth, tilts, ks, strip_rows, capacity
+):
+    outs, (lhs, wide, total, sines) = refs[: len(ks)], refs[len(ks) :]
+    step = pl.program_id(0)
+    rows, layers, width = vol_ref.shape
+    wide[...] = vol_ref[...].reshape(rows * layers, width).astype(F32)
+
+    def pair_at(z):
+        pair = [wide[pl.ds(z + h, rows, stride=layers), :].astype(BF) for h in range(2)]
+        pair = jnp.concatenate(pair, axis=1)
+        lhs[:, z * width : (z + 2) * width] = pair
+        return pair
+
+    @pl.when(step == 0)
+    def _():
+        total[...] = jnp.zeros_like(total)
+        note_sines(angle_ref, sines)
+
+    add_products(step, pair_at, total, sines, ks, tilts, layers, depth)
+
     @pl.when(step == pl.num_programs(0) - 1)
     def _():
-        _, slots = slots_of_items(row_ref, strip_rows, capacity)
-        meta = splat_rows(slots, outs[0].shape[0] - tilts * rows, width)
-        for i in range(len(ks)):
-            for t in range(tilts):
-                start = (i * tilts + t) * width
-                outs[i][t * rows : (t + 1) * rows, :] = total[:, start : start + width].astype(BF)
-            outs[i][tilts * rows :, :] = meta
+        write_slabs(row_ref, total, outs, tilts, strip_rows, capacity)
+
+
+def project_rest_kernel(
+    row_ref, angle_ref, lhs, *refs, depth, tilts, ks, layers, strip_rows, capacity
+):
+    outs, (total, sines) = refs[: len(ks)], refs[len(ks) :]
+    width = sines.shape[2]
+    total[...] = jnp.zeros_like(total)
+    note_sines(angle_ref, sines)
+
+    def some_layers(step, carry):
+        def pair_at(z):
+            start = pl.multiple_of((step * layers + z) * width, 2 * width)
+            return lhs[:, pl.ds(start, 2 * width)]
+
+        add_products(step, pair_at, total, sines, ks, tilts, layers, depth)
+        return carry
+
+    lax.fori_loop(0, depth // layers, some_layers, 0)
+    write_slabs(row_ref, total, outs, tilts, strip_rows, capacity)
 
 
 def project(volume, rows_of, angles, tilts, groups, ks, first, depth, width, strip_rows, capacity):
@@ -160,32 +179,33 @@
     layers = min(16, depth)
     length = tilts * rows + -(-tilts * rows_of.shape[1] // 16) * 16
     scalars = pl.BlockSpec(memory_space=pltpu.SMEM)
-    flat = pl.BlockSpec((rows, layers * width), lambda i: (0, i))
-    source = pl.BlockSpec((rows, layers, width), lambda i: (0, i, 0)) if first else flat
+    whole = pl.BlockSpec(memory_space=pltpu.VMEM)
+    sizes = dict(depth=depth, tilts=tilts, ks=ks, strip_rows=strip_rows, capacity=capacity)
+    slabs = [jax.ShapeDtypeStruct((length, width), BF)] * len(ks)
+    sums = [
+        pltpu.VMEM((rows, len(ks) * tilts * width), F32),
+        pltpu.VMEM((groups * tilts, 8, width), F32),
+    ]
+    if not first:
+        return pl.pallas_call(
+            functools.partial(project_rest_kernel, layers=layers, **sizes),
+            out_shape=slabs,
+            in_specs=[scalars] * 2 + [whole],
+            out_specs=[whole] * len(ks),
+            scratch_shapes=sums,
+            compiler_params=GRANT,
+            name="project_rest",
+        )(rows_of, angles, near(volume))
     return pl.pallas_call(
-        functools.partial(
-            project_kernel,
-            depth=depth,
-            tilts=tilts,
-            groups=groups,
-            ks=ks,
-            first=first,
-            strip_rows=strip_rows,
-            capacity=capacity,
-        ),
-        out_shape=[jax.ShapeDtypeStruct((length, width), BF)] * len(ks)
-        + ([jax.ShapeDtypeStruct((rows, depth * width), BF)] if first else []),
+        functools.partial(project_first_kernel, **sizes),
+        out_shape=slabs + [jax.ShapeDtypeStruct((rows, depth * width), BF)],
         grid=(depth // layers,),
-        in_specs=[scalars] * 2 + [source],
+        in_specs=[scalars] * 2 + [pl.BlockSpec((rows, layers, width), lambda i: (0, i, 0))],
         out_specs=[pl.BlockSpec((length, width), lambda i: (0, 0))] * len(ks)
-        + ([flat] if first else []),
-        scratch_shapes=([pltpu.VMEM((rows * layers, width), F32)] if first else [])
-        + [
-            pltpu.VMEM((rows, len(ks) * tilts * width), F32),
-            pltpu.VMEM((groups * tilts, 8, width), F32),
-        ],
+        + [pl.BlockSpec((rows, layers * width), lambda i: (0, i))],
+        scratch_shapes=[pltpu.VMEM((rows * layers, width), F32), *sums],
         compiler_params=GRANT,
-        name="project_first" if first else "project_rest",
+        name="project_first",
     )(rows_of, angles, volume)
 
 

time: 78.6 us -> 78.3 us (level)
  no operation moved by 1% of the time
where the time goes in v4:
time: 78.3 us; the launch traced here: 78.1 us
  Pallas kernels  30 us (38%)
  blocking collectives  20.5 us (26%)
  starting transfers between devices  15.8 us (20%)
  waiting for transfers between devices  11 us (14%)
    all_to_all x1, blocking collectives, shards(): lax.all_to_all(cuts, ('tilt', 'tile'), split_axis=0, concat_axis=0, tiled...  20.5 us
    ppermute x10, starting transfers between devices, ring(): lax.ppermute(block, axis, [(i, (i + distance) % count) for i in range(cou...  10.1 us
    pallas_call x1, Pallas kernels, back_project(): pl.pallas_call(functools.partial(back_kernel, depth=depth, tilts=tilts, b...  8.5 us
    ppermute x10, waiting for transfers between devices, ring(): lax.ppermute(block, axis, [(i, (i + distance) % count) for i in range(cou...  7.03 us
    pallas_call x1, Pallas kernels, project(): pl.pallas_call(functools.partial(project_first_kernel, **sizes), out_shap...  5.85 us
    ppermute x3, starting transfers between devices, swap(): return lax.ppermute(block, axis, [(i, i ^ distance) for i in range(count)])  5.77 us
    pallas_call x1, Pallas kernels, filter_and_cut(): pl.pallas_call(functools.partial(filter_kernel, height=height, capacity=c...  5.7 us
    pallas_call x2, Pallas kernels, project(): pl.pallas_call(functools.partial(project_rest_kernel, layers=layers, **si...  5.35 us
  transfers between devices with their start and end apart: 13, of which 10 were waited for; matrix products, arithmetic and copies ran while one was open for 0% of the time, Pallas kernels for 7%

profile of v4, /device:TPU:0, one launch (start us, length us, event | category | flops | bytes accessed | tf_op | source)
XLA Modules:
  0.0 78.1 jit_solution(14834559643961552796)
XLA Ops:
  0.6 0.0 copy-start
  0.6 5.8 %project_first.1 = (bf16[400,128]{1,0:T(8,128)(2,1)S(1)}, bf16[400,128]{1,0:T(8,128)(2,1)S(1)}, bf16[192,8192]{1,0:T(8,128)(2,1)S(1)}) custom-call(s32[2,6]{1,0:T(2,128)} %bitcast.10, f32[8]{0:T(128)} %angle_ref.7, bf16[192,64,128]{2,1,0:T(8,128)(2,1)} %bitcast.9), custom_call_target="tpu_custom_call" | custom-call | tf_op jit(solution)/shard_map/project_first/pallas_call | solution.py:199
  6.5 2.7 %project_rest.3 = bf16[400,128]{1,0:T(8,128)(2,1)S(1)} custom-call(s32[2,6]{1,0:T(2,128)} %bitcast.11, f32[8]{0:T(128)} %angle_ref.7, bf16[192,8192]{1,0:T(8,128)(2,1)S(1)} %get-tuple-element.18.lhs), custom_call_target="tpu_custom_call" | custom-call | tf_op jit(solution)/shard_map/project_rest/pallas_call | solution.py:190
  9.2 0.0 copy-start.1
  9.2 5.1 %collective-permute-start.3 = (bf16[400,128]{1,0:T(8,128)(2,1)S(1)}, bf16[400,128]{1,0:T(8,128)(2,1)S(1)}, u32[]{:S(2)}, u32[]{:S(2)}) collective-permute-start(bf16[400,128]{1,0:T(8,128)(2,1)S(1)} %project_rest.3), channel_id=1, source_target_pairs={{0,24},{8,16},{16,8},{24,0},{1,25},{9,17},{17,9},{25,1},{2,26},{10... | collective-permute-start | bytes 307208 | tf_op jit(solution)/shard_map/ppermute | solution.py:26
  14.3 0.0 collective-permute-start.1
  14.3 0.6 collective-permute-start.2
  15.0 0.0 copy-done
  15.0 1.3 %collective-permute-start = (f32[2,128,256]{2,1,0:T(8,128)S(1)}, f32[2,128,256]{2,1,0:T(8,128)S(1)}, u32[]{:S(2)}, u32[]{:S(2)}) collective-permute-start(f32[2,128,256]{2,1,0:T(8,128)S(1)} %copy-done), channel_id=1, source_target_pairs={{0,7},{1,0},{2,1},{3,2},{4,3},{5,4},{6,5},{7,6},{8,15},{9,8},{10,9... | collective-permute-start | bytes 786440 | tf_op jit(solution)/shard_map/ppermute | solution.py:20
  16.3 2.7 %project_rest.2.refs_0_ = bf16[400,128]{1,0:T(8,128)(2,1)S(1)} custom-call(s32[2,6]{1,0:T(2,128)} %bitcast.12, f32[8]{0:T(128)} %angle_ref.7, bf16[192,8192]{1,0:T(8,128)(2,1)S(1)} %get-tuple-element.18.lhs), custom_call_target="tpu_custom_call" | custom-call | tf_op jit(solution)/shard_map/project_rest/pallas_call | solution.py:190
  19.0 0.0 collective-permute-done.3.refs_3_
  19.0 1.5 %collective-permute-done.1.refs_1_ = bf16[400,128]{1,0:T(8,128)(2,1)S(1)} collective-permute-done((bf16[400,128]{1,0:T(8,128)(2,1)S(1)}, bf16[400,128]{1,0:T(8,128)(2,1)S(1)}, u32[]{:S(2)}, u32[]{:S(2)}) %collective-permute-start.1) | collective-permute-done | bytes 102432 | tf_op jit(solution)/shard_map/ppermute | solution.py:26
  20.5 2.5 %collective-permute-done.2.refs_2_ = bf16[400,128]{1,0:T(8,128)(2,1)S(1)} collective-permute-done((bf16[400,128]{1,0:T(8,128)(2,1)S(1)}, bf16[400,128]{1,0:T(8,128)(2,1)S(1)}, u32[]{:S(2)}, u32[]{:S(2)}) %collective-permute-start.2) | collective-permute-done | bytes 102432 | tf_op jit(solution)/shard_map/ppermute | solution.py:26
  22.9 1.6 %pack.1 = (bf16[336,128]{1,0:T(8,128)(2,1)S(1)}, bf16[336,128]{1,0:T(8,128)(2,1)S(1)}, bf16[336,128]{1,0:T(8,128)(2,1)S(1)}, bf16[336,128]{1,0:T(8,128)(2,1)S(1)...) custom-call(s32[2,6]{1,0:T(2,128)} %bitcast.13, ...), custom_call_target="tpu_custom_call" | custom-call | tf_op jit(solution)/shard_map/pack/pallas_call | solution.py:348
  24.5 0.1 collective-permute-start.4
  24.6 1.6 %collective-permute-start.5 = (bf16[336,128]{1,0:T(8,128)(2,1)S(1)}, bf16[336,128]{1,0:T(8,128)(2,1)S(1)}, u32[]{:S(2)}, u32[]{:S(2)}) collective-permute-start(bf16[336,128]{1,0:T(8,128)(2,1)S(1)} %get-tuple-element.23), channel_id=1, source_target_pairs={{0,2},{1,3},{2,4},{3,5},{4,6},{5,7},{6,0},{7,1},{8,10},{9,11},{10,... | collective-permute-start | bytes 258056 | tf_op jit(solution)/shard_map/ppermute | solution.py:20
  26.1 2.4 %collective-permute-start.6 = (bf16[336,128]{1,0:T(8,128)(2,1)S(1)}, bf16[336,128]{1,0:T(8,128)(2,1)S(1)}, u32[]{:S(2)}, u32[]{:S(2)}) collective-permute-start(bf16[336,128]{1,0:T(8,128)(2,1)S(1)} %get-tuple-element.24), channel_id=1, source_target_pairs={{0,3},{1,4},{2,5},{3,6},{4,7},{5,0},{6,1},{7,2},{8,11},{9,12},{10,... | collective-permute-start | bytes 258056 | tf_op jit(solution)/shard_map/ppermute | solution.py:20
  28.5 0.5 collective-permute-start.7
  29.0 0.7 collective-permute-done.4.refs_1_
  29.7 0.0 collective-permute-start.8
  29.7 1.3 %collective-permute-done.5.refs_2_ = bf16[336,128]{1,0:T(8,128)(2,1)S(1)} collective-permute-done((bf16[336,128]{1,0:T(8,128)(2,1)S(1)}, bf16[336,128]{1,0:T(8,128)(2,1)S(1)}, u32[]{:S(2)}, u32[]{:S(2)}) %collective-permute-start.5) | collective-permute-done | bytes 86048 | tf_op jit(solution)/shard_map/ppermute | solution.py:20
  31.0 1.5 %collective-permute-start.9 = (bf16[336,128]{1,0:T(8,128)(2,1)S(1)}, bf16[336,128]{1,0:T(8,128)(2,1)S(1)}, u32[]{:S(2)}, u32[]{:S(2)}) collective-permute-start(bf16[336,128]{1,0:T(8,128)(2,1)S(1)} %get-tuple-element.27), channel_id=1, source_target_pairs={{0,6},{1,7},{2,0},{3,1},{4,2},{5,3},{6,4},{7,5},{8,14},{9,15},{10,... | collective-permute-start | bytes 258056 | tf_op jit(solution)/shard_map/ppermute | solution.py:20
  32.5 1.2 %collective-permute-done.6.refs_3_ = bf16[336,128]{1,0:T(8,128)(2,1)S(1)} collective-permute-done((bf16[336,128]{1,0:T(8,128)(2,1)S(1)}, bf16[336,128]{1,0:T(8,128)(2,1)S(1)}, u32[]{:S(2)}, u32[]{:S(2)}) %collective-permute-start.6) | collective-permute-done | bytes 86048 | tf_op jit(solution)/shard_map/ppermute | solution.py:20
  33.7 0.0 collective-permute-start.10
  33.8 0.5 collective-permute-done.7.refs_4_
  34.2 0.7 collective-permute-done.8.refs_5_
  34.9 0.9 %collective-permute-done.9.refs_6_ = bf16[336,128]{1,0:T(8,128)(2,1)S(1)} collective-permute-done((bf16[336,128]{1,0:T(8,128)(2,1)S(1)}, bf16[336,128]{1,0:T(8,128)(2,1)S(1)}, u32[]{:S(2)}, u32[]{:S(2)}) %collective-permute-start.9) | collective-permute-done | bytes 86048 | tf_op jit(solution)/shard_map/ppermute | solution.py:20
  35.8 0.1 collective-permute-done.10.refs_7_
  35.9 0.0 collective-permute-done.after_ref
  35.9 1.7 %place.1 = (f32[2,288,256]{2,1,0:T(8,128)S(1)}, bf16[2,160,256]{2,1,0:T(8,128)(2,1)S(1)}, bf16[2,160,256]{2,1,0:T(8,128)(2,1)S(1)}) custom-call(f32[2,128,256]{2,1,0:T(8,128)S(1)} %copy-done, f32[2,128,256]{2,1,0:T(8,128)S(1)} %collective-permute-done.after_ref, bf16[336,128]{1,0:T(8,128)(2,1)S(1)} %get-tuple-element.21.refs_0_, ...), custom_call_target="tpu_custom_call" | custom-call | tf_op jit(solution)/shard_map/place/pallas_call | solution.py:440
  37.6 1.1 %collective-permute-start.11 = (bf16[2,160,256]{2,1,0:T(8,128)(2,1)S(1)}, bf16[2,160,256]{2,1,0:T(8,128)(2,1)S(1)}, u32[]{:S(2)}, u32[]{:S(2)}) collective-permute-start(bf16[2,160,256]{2,1,0:T(8,128)(2,1)S(1)} %get-tuple-element.30), channel_id=1, source_target_pairs={{0,1},{1,2},{2,3},{3,4},{4,5},{5,6},{6,7},{7,0},{8,9},{9,10},{10,1... | collective-permute-start | bytes 491528 | tf_op jit(solution)/shard_map/ppermute | solution.py:20
  38.7 1.6 %collective-permute-start.12 = (bf16[2,160,256]{2,1,0:T(8,128)(2,1)S(1)}, bf16[2,160,256]{2,1,0:T(8,128)(2,1)S(1)}, u32[]{:S(2)}, u32[]{:S(2)}) collective-permute-start(bf16[2,160,256]{2,1,0:T(8,128)(2,1)S(1)} %get-tuple-element.31), channel_id=1, source_target_pairs={{0,7},{1,0},{2,1},{3,2},{4,3},{5,4},{6,5},{7,6},{8,15},{9,8},{10,9... | collective-permute-start | bytes 491528 | tf_op jit(solution)/shard_map/ppermute | solution.py:20
  40.3 0.0 copy-done.1
  40.3 1.3 %transfer.1.table_ref = bf16[2,9,256,256]{3,2,1,0:T(8,128)(2,1)S(1)} custom-call(f32[2]{0:T(128)S(1)} %copy-done.1), custom_call_target="tpu_custom_call" | custom-call | tf_op jit(solution)/shard_map/transfer/pallas_call | solution.py:495
  41.6 1.7 %collective-permute-done.11.above_ref = bf16[2,160,256]{2,1,0:T(8,128)(2,1)S(1)} collective-permute-done((bf16[2,160,256]{2,1,0:T(8,128)(2,1)S(1)}, bf16[2,160,256]{2,1,0:T(8,128)(2,1)S(1)}, u32[]{:S(2)}, u32[]{:S(2)}) %collective-permute-start.11) | collective-permute-done | bytes 163872 | tf_op jit(solution)/shard_map/ppermute | solution.py:20
  43.4 0.0 collective-permute-done.12.below_ref
  43.4 5.7 %filter_and_cut.1 = (f32[2,128,256]{2,1,0:T(8,128)}, bf16[4,8,64,128]{3,2,1,0:T(8,128)(2,1)S(1)}) custom-call(f32[2,288,256]{2,1,0:T(8,128)S(1)} %get-tuple-element.29.canvas_ref, bf16[2,160,256]{2,1,0:T(8,128)(2,1)S(1)} %collective-permute-done.11.above_ref, bf16[2,160,256]{2,1,0:T(8,128)(2,1)S(1)} %collective-permute-done.12.below_ref, ...), custom_call_target="tpu_custom_call" | custom-call | tf_op jit(solution)/shard_map/filter_and_cut/pallas_call | solution.py:592
  49.1 20.5 %all_to_all.5 = bf16[32,64,128]{2,1,0:T(8,128)(2,1)S(1)} all-to-all(bf16[32,64,128]{2,1,0:T(8,128)(2,1)S(1)} %bitcast.7), channel_id=1, replica_groups=mesh['tilt'=4,'tile'=8] {'tilt','tile'}, dimensions={0} | all-to-all | bytes 1048576 | tf_op jit(solution)/shard_map/all_to_all | solution.py:637
  69.6 8.5 %back_project.1 = f32[192,64,128]{2,1,0:T(8,128)} custom-call(f32[8]{0:T(128)} %angle_ref.7, bf16[4,512,128]{2,1,0:T(8,128)(2,1)S(1)} %bitcast.6, bf16[400,128]{1,0:T(8,128)(2,1)S(1)} %project_rest.2.refs_0_, bf16[400,128]{1,0:T(8,128)(2,1)S(1)} %collective-permute-done.1.refs_1_, bf16[400,128]{1,0:T(8,128)(2,1)S(1)} %collective-permute-done.2.refs_2_, ...), custom_call_target="tpu_custom_call" | custom-call | tf_op jit(solution)/shard_map/back_project/pallas_call | solution.py:266
Async XLA Ops:
  0.6 14.3 %copy-start = (f32[2,128,256]{2,1,0:T(8,128)S(1)}, f32[2,128,256]{2,1,0:T(8,128)}, u32[]{:S(2)}) copy-start(f32[2,128,256]{2,1,0:T(8,128)} %measured_ref.3) | copy-start | bytes 786436
  9.2 31.1 %copy-start.1 = (f32[2]{0:T(128)S(1)}, f32[2]{0:T(128)}, u32[]{:S(2)}) copy-start(f32[2]{0:T(128)} %defocus_ref.1) | copy-start | bytes 28
  9.2 9.8 %collective-permute-start.3 = (bf16[400,128]{1,0:T(8,128)(2,1)S(1)}, bf16[400,128]{1,0:T(8,128)(2,1)S(1)}, u32[]{:S(2)}, u32[]{:S(2)}) collective-permute-start(bf16[400,128]{1,0:T(8,128)(2,1)S(1)} %project_rest.3), channel_id=1, source_target_pairs={{0,24},{8,16},{16,8},{24,0},{1,25},{9,17},{17,9},{25,1},{2,26},{10... | collective-permute-start | bytes 307208 | tf_op jit(solution)/shard_map/ppermute | solution.py:26
  14.3 6.1 %collective-permute-start.1 = (bf16[400,128]{1,0:T(8,128)(2,1)S(1)}, bf16[400,128]{1,0:T(8,128)(2,1)S(1)}, u32[]{:S(2)}, u32[]{:S(2)}) collective-permute-start(bf16[400,128]{1,0:T(8,128)(2,1)S(1)} %get-tuple-element.19), channel_id=1, source_target_pairs={{0,8},{8,0},{16,24},{24,16},{1,9},{9,1},{17,25},{25,17},{2,10},{10... | collective-permute-start | bytes 307208 | tf_op jit(solution)/shard_map/ppermute | solution.py:26
  14.3 8.6 %collective-permute-start.2 = (bf16[400,128]{1,0:T(8,128)(2,1)S(1)}, bf16[400,128]{1,0:T(8,128)(2,1)S(1)}, u32[]{:S(2)}, u32[]{:S(2)}) collective-permute-start(bf16[400,128]{1,0:T(8,128)(2,1)S(1)} %get-tuple-element.20), channel_id=1, source_target_pairs={{0,16},{8,24},{16,0},{24,8},{1,17},{9,25},{17,1},{25,9},{2,18},{10... | collective-permute-start | bytes 307208 | tf_op jit(solution)/shard_map/ppermute | solution.py:26
  15.0 20.9 %collective-permute-start = (f32[2,128,256]{2,1,0:T(8,128)S(1)}, f32[2,128,256]{2,1,0:T(8,128)S(1)}, u32[]{:S(2)}, u32[]{:S(2)}) collective-permute-start(f32[2,128,256]{2,1,0:T(8,128)S(1)} %copy-done), channel_id=1, source_target_pairs={{0,7},{1,0},{2,1},{3,2},{4,3},{5,4},{6,5},{7,6},{8,15},{9,8},{10,9... | collective-permute-start | bytes 786440 | tf_op jit(solution)/shard_map/ppermute | solution.py:20
  24.5 5.2 %collective-permute-start.4 = (bf16[336,128]{1,0:T(8,128)(2,1)S(1)}, bf16[336,128]{1,0:T(8,128)(2,1)S(1)}, u32[]{:S(2)}, u32[]{:S(2)}) collective-permute-start(bf16[336,128]{1,0:T(8,128)(2,1)S(1)} %get-tuple-element.22), channel_id=1, source_target_pairs={{0,1},{1,2},{2,3},{3,4},{4,5},{5,6},{6,7},{7,0},{8,9},{9,10},{10,1... | collective-permute-start | bytes 258056 | tf_op jit(solution)/shard_map/ppermute | solution.py:20
  24.6 6.4 %collective-permute-start.5 = (bf16[336,128]{1,0:T(8,128)(2,1)S(1)}, bf16[336,128]{1,0:T(8,128)(2,1)S(1)}, u32[]{:S(2)}, u32[]{:S(2)}) collective-permute-start(bf16[336,128]{1,0:T(8,128)(2,1)S(1)} %get-tuple-element.23), channel_id=1, source_target_pairs={{0,2},{1,3},{2,4},{3,5},{4,6},{5,7},{6,0},{7,1},{8,10},{9,11},{10,... | collective-permute-start | bytes 258056 | tf_op jit(solution)/shard_map/ppermute | solution.py:20
  26.1 7.6 %collective-permute-start.6 = (bf16[336,128]{1,0:T(8,128)(2,1)S(1)}, bf16[336,128]{1,0:T(8,128)(2,1)S(1)}, u32[]{:S(2)}, u32[]{:S(2)}) collective-permute-start(bf16[336,128]{1,0:T(8,128)(2,1)S(1)} %get-tuple-element.24), channel_id=1, source_target_pairs={{0,3},{1,4},{2,5},{3,6},{4,7},{5,0},{6,1},{7,2},{8,11},{9,12},{10,... | collective-permute-start | bytes 258056 | tf_op jit(solution)/shard_map/ppermute | solution.py:20
  28.5 5.7 %collective-permute-start.7 = (bf16[336,128]{1,0:T(8,128)(2,1)S(1)}, bf16[336,128]{1,0:T(8,128)(2,1)S(1)}, u32[]{:S(2)}, u32[]{:S(2)}) collective-permute-start(bf16[336,128]{1,0:T(8,128)(2,1)S(1)} %get-tuple-element.25), channel_id=1, source_target_pairs={{0,4},{1,5},{2,6},{3,7},{4,0},{5,1},{6,2},{7,3},{8,12},{9,13},{10,... | collective-permute-start | bytes 258056 | tf_op jit(solution)/shard_map/ppermute | solution.py:20
  29.7 5.2 %collective-permute-start.8 = (bf16[336,128]{1,0:T(8,128)(2,1)S(1)}, bf16[336,128]{1,0:T(8,128)(2,1)S(1)}, u32[]{:S(2)}, u32[]{:S(2)}) collective-permute-start(bf16[336,128]{1,0:T(8,128)(2,1)S(1)} %get-tuple-element.26), channel_id=1, source_target_pairs={{0,5},{1,6},{2,7},{3,0},{4,1},{5,2},{6,3},{7,4},{8,13},{9,14},{10,... | collective-permute-start | bytes 258056 | tf_op jit(solution)/shard_map/ppermute | solution.py:20
  31.0 4.8 %collective-permute-start.9 = (bf16[336,128]{1,0:T(8,128)(2,1)S(1)}, bf16[336,128]{1,0:T(8,128)(2,1)S(1)}, u32[]{:S(2)}, u32[]{:S(2)}) collective-permute-start(bf16[336,128]{1,0:T(8,128)(2,1)S(1)} %get-tuple-element.27), channel_id=1, source_target_pairs={{0,6},{1,7},{2,0},{3,1},{4,2},{5,3},{6,4},{7,5},{8,14},{9,15},{10,... | collective-permute-start | bytes 258056 | tf_op jit(solution)/shard_map/ppermute | solution.py:20
  33.7 2.1 %collective-permute-start.10 = (bf16[336,128]{1,0:T(8,128)(2,1)S(1)}, bf16[336,128]{1,0:T(8,128)(2,1)S(1)}, u32[]{:S(2)}, u32[]{:S(2)}) collective-permute-start(bf16[336,128]{1,0:T(8,128)(2,1)S(1)} %get-tuple-element.28), channel_id=1, source_target_pairs={{0,7},{1,0},{2,1},{3,2},{4,3},{5,4},{6,5},{7,6},{8,15},{9,8},{10,9... | collective-permute-start | bytes 258056 | tf_op jit(solution)/shard_map/ppermute | solution.py:20
  37.6 5.8 %collective-permute-start.11 = (bf16[2,160,256]{2,1,0:T(8,128)(2,1)S(1)}, bf16[2,160,256]{2,1,0:T(8,128)(2,1)S(1)}, u32[]{:S(2)}, u32[]{:S(2)}) collective-permute-start(bf16[2,160,256]{2,1,0:T(8,128)(2,1)S(1)} %get-tuple-element.30), channel_id=1, source_target_pairs={{0,1},{1,2},{2,3},{3,4},{4,5},{5,6},{6,7},{7,0},{8,9},{9,10},{10,1... | collective-permute-start | bytes 491528 | tf_op jit(solution)/shard_map/ppermute | solution.py:20
  38.7 4.7 %collective-permute-start.12 = (bf16[2,160,256]{2,1,0:T(8,128)(2,1)S(1)}, bf16[2,160,256]{2,1,0:T(8,128)(2,1)S(1)}, u32[]{:S(2)}, u32[]{:S(2)}) collective-permute-start(bf16[2,160,256]{2,1,0:T(8,128)(2,1)S(1)} %get-tuple-element.31), channel_id=1, source_target_pairs={{0,7},{1,0},{2,1},{3,2},{4,3},{5,4},{6,5},{7,6},{8,15},{9,8},{10,9... | collective-permute-start | bytes 491528 | tf_op jit(solution)/shard_map/ppermute | solution.py:20
